TPU v7x, 32 devices: a whole 2x2x4 slice. The times are simulated.
32 devices in a mesh: rows: 8 (over y, x, core), rhs: 4 (over z).
Axes of the slice: x: 2, y: 2, z: 4, core: 2. Of those that a mesh axis runs over, the one named last changes fastest.
Arguments:
- win_rows: bfloat16 [4096, 4096], P('rows'), may hold values from -0.09375 to 0.09375
- anc_rows: bfloat16 [16384, 4096], P('rows'), may hold values from -0.09375 to 0.09375
- win_pattern: int32 [64, 64], replicated, may hold values 0 or 1
- anc_pattern: int32 [256, 64], P('rows'), may hold values 0 or 1
- window_owner: int32 [64], replicated, may hold values from 0 to 63, each once
- sn_order: int32 [8], replicated, may hold values from 0 to 7, each once
- diag_inv: bfloat16 [8, 512, 512], replicated, as said below
- rhs_win: bfloat16 [4096, 1024], P(('rows', 'rhs')), may hold values from -0.119628906 to 0.119628906
- rhs_anc: bfloat16 [16384, 1024], P(('rows', 'rhs')), may hold values from -6 to 6
Outputs:
- window_solution: bfloat16 [4096, 1024], P(None, 'rhs')
- anc_residual: bfloat16 [16384, 1024], P('rows', 'rhs')
Inputs may be any that keep to these rules, and one draw needn't show every extreme that they name: `window_owner`: each storage slot holds exactly one window block row. `sn_order`: each supernode label appears once. `diag_inv`: each block is lower triangular.
All inputs are finite; a program needn't handle non-finite values. No bound on the sum of `anc_pattern` on one device may be relied on, other than what follows from the above.
Results may differ from a plain program's by a relative error of at most 0.025.
Values may be sent and summed in bfloat16 or wider, within the bound.
No kernel may reach another device: no remote copies, remote signals or barrier semaphores. Data moves between devices by JAX's collectives and lax.ppermute only.
A program may use at most 256 MiB of HBM per device.

v0:
```python
import jax
import jax.numpy as jnp
from jax import lax
from jax.experimental import pallas as pl
from jax.experimental.pallas import tpu as pltpu
from jax.sharding import PartitionSpec as P

BS = 64
SB = 8
NSUP = 8
SN = 512
NW = 4096
NWB = 64
GROUPS = 4
PAIR = 2 * SN
F32 = jnp.float32
BF16 = jnp.bfloat16


def masked_columns(factor, pattern, node_label):
    blocks = pattern.shape[0]
    columns = lax.dynamic_slice_in_dim(factor, node_label * SN, SN, 1)
    chosen = lax.dynamic_slice_in_dim(pattern, node_label * SB, SB, 1)
    shaped = columns.reshape(blocks, BS, SB, BS) * chosen[:, None, :, None].astype(BF16)
    return shaped.reshape(blocks * BS, SN)


def sum_over_rows(values):
    count = lax.axis_size("rows")
    if count & (count - 1):
        return lax.psum(values, "rows")
    step = 1
    while step < count:
        values = values + lax.ppermute(values, "rows", [(i, i ^ step) for i in range(count)])
        step *= 2
    return values


def general_path(win_rows, anc_rows, win_pattern, anc_pattern, window_owner, sn_order, diag_inv, win_rhs, anc_rhs):
    columns_rhs = win_rhs.shape[1]
    slot_count = win_rows.shape[0] // BS
    first_slot = lax.axis_index("rows") * slot_count
    local_pattern = lax.dynamic_slice_in_dim(win_pattern, first_slot, slot_count, 0)

    def step(position, carry):
        solution, win_resid, anc_resid = carry
        node_label = sn_order[position]
        owners = lax.dynamic_slice_in_dim(window_owner, node_label * SB, SB, 0)
        inverse = lax.dynamic_index_in_dim(diag_inv, node_label, 0, keepdims=False)
        local_place = owners - first_slot
        present = (local_place >= 0) & (local_place < slot_count)
        resid_blocks = win_resid.reshape(slot_count, BS, columns_rhs)
        taken = jnp.take(resid_blocks, jnp.clip(local_place, 0, slot_count - 1), axis=0)
        placed = jnp.where(present[:, None, None], taken, 0.0).reshape(SN, columns_rhs)
        panel = sum_over_rows(placed.astype(BF16))
        solved = jnp.dot(inverse, panel, preferred_element_type=F32).astype(BF16)
        solution = lax.dynamic_update_slice_in_dim(solution, solved, node_label * SN, 0)
        win_part = jnp.dot(masked_columns(win_rows, local_pattern, node_label), solved, preferred_element_type=F32)
        anc_part = jnp.dot(masked_columns(anc_rows, anc_pattern, node_label), solved, preferred_element_type=F32)
        return solution, win_resid - win_part, anc_resid - anc_part

    first = (jnp.zeros((NW, columns_rhs), BF16), win_rhs.astype(F32), anc_rhs.astype(F32))
    solution, _, anc_resid = lax.fori_loop(0, NSUP, step, first)
    return solution, anc_resid.astype(BF16)


def spread_matrix():
    block_index = lax.broadcasted_iota(jnp.int32, (NWB, SN), 0)
    lane_index = lax.broadcasted_iota(jnp.int32, (NWB, SN), 1)
    return ((block_index & 7) == (lane_index >> 6)).astype(F32).astype(BF16)


def expand_mask(rows_pattern, label, spread):
    lane = lax.broadcasted_iota(jnp.int32, rows_pattern.shape, 1)
    chosen = jnp.where((lane >> 3) == label, rows_pattern, 0).astype(F32).astype(BF16)
    return jnp.dot(chosen, spread, preferred_element_type=F32).astype(BF16)


def masked_rows(block_of, mask, count):
    return jnp.concatenate([block_of(j) * mask[j:j + 1, :] for j in range(count)], axis=0)


def rows_at(index):
    return pl.ds(pl.multiple_of(index * BS, BS), BS)


def columns_at(label):
    return pl.ds(pl.multiple_of(label * SN, SN), SN)


SRC, LSRC, PACK, TABLE = 0, 64, 96, 128


def factor_kernel(owner, order, pattern, win_ref, out, buf, pat, inv, pos, sem):
    row = lax.axis_index("rows")

    for w in range(NWB):
        slot = owner[w]
        inv[jnp.where((slot >> 3) == row, (slot & 7), SB)] = w
    for k in range(NSUP):
        pos[order[k]] = k
    labels = jnp.zeros((SB, 1), jnp.int32)
    for t in range(SB):
        label = order[(pos[(inv[t] >> 3)] // 2) * 2]
        pltpu.make_async_copy(win_ref.at[pl.ds(t * BS, BS), columns_at(label)], buf.at[pl.ds(t * BS, BS), :], sem).start()
        labels = jnp.where(lax.broadcasted_iota(jnp.int32, (SB, 1), 0) == t, label, labels)
    pat[...] = pattern[pl.ds(pl.multiple_of(row * SB, SB), SB), :]
    mask = expand_mask(pat[...], labels, spread_matrix())
    pltpu.make_async_copy(win_ref.at[:, pl.ds(0, SN)], buf, sem).wait()
    for j in range(SB):
        out[j * BS:(j + 1) * BS, :] = buf[j * BS:(j + 1) * BS, :] * mask[j:j + 1, :]


def rhs_pack_kernel(rhs_ref, *sent):
    depth = lax.axis_index("rhs")
    width = sent[0].shape[1]
    for s, out in enumerate(sent):
        at = pl.multiple_of(jnp.bitwise_xor(depth, s) * width, width)
        out[...] = rhs_ref[:, pl.ds(at, width)]


def chip_pack_kernel(own_ref, other_ref, l_chip):
    l_chip[0:SN, :] = own_ref[...]
    l_chip[SN:PAIR, :] = other_ref[...]


def take_half_kernel(x_ref, out):
    out[...] = x_ref[0:SN, :]


def table_kernel(owner, order, tab, flag):
    row = lax.axis_index("rows")
    chip, core = (row >> 1), (row & 1)
    bad = 0
    for t in range(GROUPS * SB):
        tab[PACK + t] = 0
    for group in range(GROUPS):
        counts = 0
        for i in range(2 * SB):
            slot = owner[order[2 * group + (i >> 3)] * SB + (i & 7)]
            where, device = (slot >> 4), (slot >> 3)
            rank = (counts >> (8 * where)) & 255
            counts = counts + (1 << (8 * where))
            bad = bad | ((rank >> 3))
            rank = jnp.minimum(rank, SB - 1)
            rel = jnp.bitwise_xor(where, chip)
            cross = jnp.bitwise_xor((device & 1), core)
            kind = jnp.where((rel == 1) | (rel == 2), jnp.where(rel == 1 + core, 1, 2), rel)
            far_rank = 3 * SB + jnp.where((rank >> 2) == core, 0, 4) + (rank & 3)
            tab[SRC + group * 16 + i] = jnp.where(kind == 3, far_rank, kind * SB + rank)
            tab[jnp.where(rel == 0, PACK + group * SB + rank, TABLE)] = cross * SB + (slot & 7)
            if i >= SB:
                tab[LSRC + group * SB + i - SB] = (2 * kind + cross) * SB + (slot & 7)
    flag[0] = bad
    flag[1] = lax.axis_index("rhs")


def below_rhs_kernel(rhs_ref, *outs):
    depth = lax.axis_index("rhs")
    width = outs[0].shape[1]
    for s, out in enumerate(outs):
        out[...] = rhs_ref[:, pl.ds(pl.multiple_of(jnp.bitwise_xor(depth, s) * width, width), width)]


def first_pack_kernel(owner, order, *refs):
    pieces, (chip_rhs, p_ref, b_ref, place) = refs[:8], refs[8:]
    row, depth = lax.axis_index("rows"), lax.axis_index("rhs")
    core = (row & 1)
    tall = pieces[0].shape[0]
    for side in range(2):
        for s in range(4):
            at = pl.multiple_of(side * SB * BS + jnp.bitwise_xor(depth, s) * tall, tall)
            chip_rhs[pl.ds(at, tall), :] = pieces[4 * side + s][...]
    for t in range(SB):
        place[t] = 0
    rank = 0
    for i in range(2 * SB):
        slot = owner[order[(i >> 3)] * SB + (i & 7)]
        here = (slot >> 4) == (row >> 1)
        place[jnp.where(here & (rank < SB), rank, SB)] = jnp.bitwise_xor(((slot >> 3) & 1), core) * SB + (slot & 7)
        rank = rank + jnp.where(here, 1, 0)
    for t in range(SB):
        p_ref[t * BS:(t + 1) * BS, :] = chip_rhs[rows_at(place[t]), :]
    b_ref[...] = p_ref[pl.ds(pl.multiple_of(core * (SB >> 1) * BS, (SB >> 1) * BS), (SB >> 1) * BS), :]


def make_mask_kernel(group):
    def kernel(tab, order, pattern, w_own, w_other, out, pat):
        row = lax.axis_index("rows")
        places = [tab[PACK + (group + 1) * SB + j] for j in range(SB)]
        for j, place in enumerate(places):
            pat[j:j + 1, :] = pattern[pl.ds(jnp.bitwise_xor(row, (place >> 3)) * SB + (place & 7), 1), :]
        spread = spread_matrix()
        rows = pat[...]
        masks = [expand_mask(rows, order[k], spread) for k in range(2 * group + 2)]
        for j, place in enumerate(places):
            at = slice(j * BS, (j + 1) * BS)
            for side, w_ref in enumerate((w_own, w_other)):
                @pl.when((place >> 3) == side)
                def _(w_ref=w_ref, at=at, j=j, place=place):
                    for k in range(2 * group + 2):
                        block = w_ref[rows_at((place & 7)), columns_at(order[k])]
                        out[at, k * SN:(k + 1) * SN] = block * masks[k][j:j + 1, :]

    return kernel


def make_prep_kernel(group):
    last = group == GROUPS - 1

    def kernel(tab, order, diag, *refs):
        own, other, near, near_swap, far, far_swap = refs[:6]
        l_refs = ((own, 0), (other, 0), (near, 0), (near, SB), (near_swap, SB), (near_swap, 0), (far, 0), (far_swap, 0))
        refs = refs[6:]
        if last:
            m_out, lbuf = refs
        else:
            w_ref, chip_rhs = refs[:2]
            xs = refs[2:2 + group]
            m_out, r_out, lbuf = refs[2 + group:]
        for i in range(SB):
            code = tab[LSRC + group * SB + i]
            for m in range(8):
                @pl.when((code >> 3) == m)
                def _(m=m, i=i, code=code):
                    lbuf[i * BS:(i + 1) * BS, :] = l_refs[m][0][rows_at((code & 7) + l_refs[m][1]), :]
        first, second = diag[order[2 * group]], diag[order[2 * group + 1]]
        m_out[0:SN, 0:SN] = first
        m_out[SN:PAIR, SN:PAIR] = second
        joined = jnp.dot(second, lbuf[...], preferred_element_type=F32).astype(BF16)
        m_out[SN:PAIR, 0:SN] = (-jnp.dot(joined, first, preferred_element_type=F32)).astype(BF16)
        if not last:
            total = jnp.concatenate([chip_rhs[rows_at(tab[PACK + (group + 1) * SB + j]), :] for j in range(SB)], axis=0).astype(F32)
            for k in range(group):
                total = total - jnp.dot(w_ref[:, k * PAIR:(k + 1) * PAIR], xs[k][...], preferred_element_type=F32)
            r_out[...] = total

    return kernel


def make_solve_kernel(group):
    last = group == GROUPS - 1

    def kernel(*refs):
        tab, sources, m_ref = refs[0], refs[1:6], refs[6]
        if last:
            x_ref, panel, pool = refs[7:]
        else:
            r_ref, wn_ref, x_ref, p_ref, b_ref, panel, pool = refs[7:]
        at = 0
        for source in sources:
            pool[at:at + source.shape[0], :] = source[...]
            at += source.shape[0]
        for i in range(2 * SB):
            panel[i * BS:(i + 1) * BS, :] = pool[rows_at(tab[SRC + group * 16 + i]), :]
        x_ref[0:SN, :] = jnp.dot(m_ref[0:SN, 0:SN], panel[0:SN, :], preferred_element_type=F32).astype(BF16)
        x_ref[SN:PAIR, :] = jnp.dot(m_ref[SN:PAIR, :], panel[...], preferred_element_type=F32).astype(BF16)
        if last:
            return
        total = r_ref[...] - jnp.dot(wn_ref[:, group * PAIR:(group + 1) * PAIR], x_ref[...], preferred_element_type=F32)
        p_ref[...] = total.astype(BF16)
        core = lax.axis_index("rows") % 2
        b_ref[...] = p_ref[pl.ds(pl.multiple_of(core * (SB >> 1) * BS, (SB >> 1) * BS), (SB >> 1) * BS), :]

    return kernel


def make_below_mask_kernel(tile):
    def kernel(pattern, a_ref, out, sems):
        copies = []
        count = 2 * SB
        for j in range(count):
            c = pltpu.make_async_copy(a_ref.at[pl.ds((tile * count + j) * BS, BS), :], out.at[pl.ds(j * BS, BS), :], sems.at[j])
            c.start()
            copies.append(c)
        spread = spread_matrix()
        rows = pattern[tile * count:(tile + 1) * count, :]
        masks = [expand_mask(rows, k, spread) for k in range(NSUP)]
        for j in range(count):
            copies[j].wait()
            for k in range(NSUP):
                at = (slice(j * BS, (j + 1) * BS), slice(k * SN, (k + 1) * SN))
                out[at] = out[at] * masks[k][j:j + 1, :]

    return kernel


def below_product(order, a_ref, x_ref, group, i):
    rows = slice(((i & 1)) * SN, ((i & 1) + 1) * SN)
    first = jnp.dot(a_ref[rows, columns_at(order[2 * group])], x_ref[0:SN, :], preferred_element_type=F32)
    return first + jnp.dot(a_ref[rows, columns_at(order[2 * group + 1])], x_ref[SN:PAIR, :], preferred_element_type=F32)


def two_rows_kernel(order, a0, a1, x0_ref, x1_ref, out):
    for i, a_ref in enumerate((a0, a0, a1, a1)):
        out[i * SN:(i + 1) * SN, :] = below_product(order, a_ref, x0_ref, 0, i) + below_product(order, a_ref, x1_ref, 1, i)


def base_rows_kernel(order, a0, a1, x_ref, sums, h0, h1, h2, h3, out, rhs):
    depth = lax.axis_index("rhs")
    tall = h0.shape[0]
    for s, h in enumerate((h0, h1, h2, h3)):
        rhs[pl.ds(pl.multiple_of(jnp.bitwise_xor(depth, s) * tall, tall), tall), :] = h[...]
    for i, a_ref in enumerate((a0, a0, a1, a1)):
        at = slice(i * SN, (i + 1) * SN)
        out[at, :] = rhs[at, :].astype(F32) - (sums[at, :] + below_product(order, a_ref, x_ref, 2, i))


def last_rows_kernel(order, a0, a1, x0, x1, x2, x3, base, sol_ref, out_ref, done, sems, osem):
    copies = []
    for k, x in enumerate((x0, x1, x2, x3)):
        for q in range(2):
            at = pl.multiple_of(order[2 * k + q] * SN, SN)
            copies.append(pltpu.make_async_copy(x.at[pl.ds(q * SN, SN), :], sol_ref.at[pl.ds(at, SN), :], sems.at[2 * k + q]))
            copies[-1].start()
    for i, a_ref in enumerate((a0, a0, a1, a1)):
        at = slice(i * SN, (i + 1) * SN)
        done[at, :] = (base[at, :] - below_product(order, a_ref, x3, GROUPS - 1, i)).astype(BF16)
        copies.append(pltpu.make_async_copy(done.at[pl.ds(i * SN, SN), :], out_ref.at[pl.ds(i * SN, SN), :], osem.at[i]))
        copies[-1].start()
    for c in copies:
        c.wait()


def in_vmem(x):
    return pltpu.with_memory_space_constraint(x, pltpu.VMEM)


def in_hbm(x):
    return pltpu.with_memory_space_constraint(x, pltpu.HBM)


SMEM = pl.BlockSpec(memory_space=pltpu.SMEM)
VMEM = pl.BlockSpec(memory_space=pltpu.VMEM)
HBM = pl.BlockSpec(memory_space=pltpu.HBM)


def params(mib):
    return pltpu.CompilerParams(vmem_limit_bytes=mib * 1024 * 1024)


def cost(micros):
    return pl.CostEstimate(flops=micros * 10 ** 8, bytes_accessed=micros * 3 * 10 ** 6, transcendentals=0)


def shape_of(dims, dtype=BF16):
    return jax.ShapeDtypeStruct(dims, dtype)


def local(win_rows, anc_rows, win_pattern, anc_pattern, window_owner, sn_order, diag_inv, rhs_win, rhs_anc):
    if lax.axis_size("rows") != 8 or lax.axis_size("rhs") != 4 or anc_rows.shape[0] != 4 * SB * BS:
        win_rhs = lax.all_to_all(rhs_win, "rhs", split_axis=1, concat_axis=0, tiled=True)
        anc_rhs = lax.all_to_all(rhs_anc, "rhs", split_axis=1, concat_axis=0, tiled=True)
        return general_path(win_rows, anc_rows, win_pattern, anc_pattern, window_owner, sn_order, diag_inv, win_rhs, anc_rhs)

    def swap(x, m):
        return lax.ppermute(x, "rows", [(i, i ^ m) for i in range(8)])

    def deep(x, m):
        return lax.ppermute(x, "rhs", [(i, i ^ m) for i in range(4)])

    def neighbour(x):
        return lax.ppermute(x, "rows", [(i, i ^ (2 if i % 2 == 0 else 4)) for i in range(8)])

    def forward(x):
        return lax.ppermute(x, "rows", [(i, i ^ (4 if i % 2 == 0 else 2)) for i in range(8)])

    def mask_below(k, after):
        pattern_later, _ = lax.optimization_barrier((anc_pattern, after))
        return pl.pallas_call(
            make_below_mask_kernel(k),
            out_shape=shape_of((PAIR, NW)),
            in_specs=[VMEM, HBM],
            out_specs=VMEM,
            scratch_shapes=[pltpu.SemaphoreType.DMA((2 * SB,))],
            compiler_params=params(4),
            cost_estimate=cost(4),
            name="mask_below",
        )(pattern_later, in_hbm(anc_rows))

    columns = rhs_win.shape[1] // 4
    half = SN // 2
    tall = rhs_win.shape[0]
    w_own = in_hbm(win_rows)
    l_own = pl.pallas_call(
        factor_kernel,
        out_shape=shape_of((SN, SN)),
        in_specs=[SMEM, SMEM, VMEM, HBM],
        out_specs=VMEM,
        scratch_shapes=[pltpu.VMEM((SN, SN), BF16), pltpu.VMEM((SB, NWB), jnp.int32),
                        pltpu.SMEM((SB + 1,), jnp.int32), pltpu.SMEM((SB,), jnp.int32), pltpu.SemaphoreType.DMA],
        compiler_params=params(4),
        cost_estimate=cost(2),
        name="factor_pack",
    )(window_owner, sn_order, win_pattern, w_own)
    l_other = swap(l_own, 1)
    l_chip = pl.pallas_call(
        chip_pack_kernel,
        out_shape=shape_of((PAIR, SN)),
        in_specs=[VMEM] * 2,
        out_specs=VMEM,
        compiler_params=params(4),
        cost_estimate=cost(1),
        name="chip_pack",
    )(l_own, l_other)
    near = neighbour(l_chip)
    rhs_late, _ = lax.optimization_barrier((rhs_win, l_chip))
    sent = pl.pallas_call(
        rhs_pack_kernel,
        out_shape=(shape_of((tall, columns)),) * 4,
        in_specs=[VMEM],
        out_specs=(VMEM,) * 4,
        compiler_params=params(4),
        cost_estimate=cost(1),
        name="rhs_pack",
    )(rhs_late)
    pieces = [sent[0]] + [deep(sent[s], s) for s in (1, 2, 3)]
    w_late, _ = lax.optimization_barrier((win_rows, l_chip))
    w_other = swap(w_late, 1)
    below = [mask_below(0, l_chip)]
    w_other, below[0], *pieces = lax.optimization_barrier((w_other, *below, *pieces))
    others = [swap(x, 1) for x in pieces]
    chip_rhs, packed, part = pl.pallas_call(
        first_pack_kernel,
        out_shape=(shape_of((PAIR, columns)), shape_of((SN, columns)), shape_of((half, columns))),
        in_specs=[SMEM, SMEM] + [VMEM] * 8,
        out_specs=(VMEM,) * 3,
        scratch_shapes=[pltpu.SMEM((SB + 1,), jnp.int32)],
        compiler_params=params(4),
        cost_estimate=cost(1),
        name="first_pack",
    )(window_owner, sn_order, *pieces, *others)
    near, _ = lax.optimization_barrier((near, packed))
    near_half = pl.pallas_call(
        take_half_kernel,
        out_shape=shape_of((SN, SN)),
        in_specs=[VMEM],
        out_specs=VMEM,
        compiler_params=params(4),
        cost_estimate=cost(1),
        name="take_half",
    )(near)
    far = forward(near_half)
    owner_later, order_later, _ = lax.optimization_barrier((window_owner, sn_order, packed))
    tab, flag = pl.pallas_call(
        table_kernel,
        out_shape=(shape_of((TABLE + 1,), jnp.int32), shape_of((2,), jnp.int32)),
        in_specs=[SMEM, SMEM],
        out_specs=(SMEM, SMEM),
        compiler_params=params(4),
        cost_estimate=cost(2),
        name="tables",
    )(owner_later, order_later)
    w_other = in_vmem(w_other)
    w_own = in_vmem(win_rows)

    tile = rhs_anc.shape[0]
    sums, solved, masked = None, [], []
    diag_vmem = in_vmem(diag_inv)
    below_rows = anc_rows.shape[0]

    anc_order, anc_pieces = (2, 3, 1), [None] * 4
    for group in range(GROUPS):
        last = group == GROUPS - 1
        a_own = neighbour(packed)
        b_own = swap(part, 6)
        if group == 0:
            for k in range(GROUPS - 1):
                masked.append(pl.pallas_call(
                    make_mask_kernel(k),
                    out_shape=shape_of((SN, (k + 1) * PAIR)),
                    in_specs=[SMEM, SMEM, VMEM, VMEM, VMEM],
                    out_specs=VMEM,
                    scratch_shapes=[pltpu.VMEM((SB, NWB), jnp.int32)],
                    compiler_params=params(6),
                    cost_estimate=cost(2),
                    name="mask_rows",
                )(tab, order_later, win_pattern, w_own, w_other))
        if group == 0:
            rhs_later, _ = lax.optimization_barrier((rhs_anc, packed))
            anc_pieces = list(pl.pallas_call(
                below_rhs_kernel,
                out_shape=(shape_of((tile, columns)),) * 4,
                in_specs=[VMEM],
                out_specs=(VMEM,) * 4,
                compiler_params=params(4),
                cost_estimate=cost(1),
                name="below_rhs",
            )(in_vmem(rhs_later)))
        if not last:
            s = anc_order[group]
            moved, _ = lax.optimization_barrier((anc_pieces[s], packed))
            anc_pieces[s] = deep(moved, s)

        if group == 0:
            a_own, b_own, near, far, *masked = lax.optimization_barrier(
                (a_own, b_own, near, far, *masked))
            l_parts = [in_vmem(x) for x in (l_own, l_other, near, swap(near, 1), far, swap(far, 1))]
        operands = [tab, sn_order, diag_vmem, *l_parts]
        out_shape = [shape_of((PAIR, PAIR))]
        if not last:
            operands += [masked[group], chip_rhs, *solved]
            out_shape += [shape_of((SN, columns), F32)]
        ready = pl.pallas_call(
            make_prep_kernel(group),
            out_shape=tuple(out_shape),
            in_specs=[SMEM, SMEM] + [VMEM] * (len(operands) - 2),
            out_specs=(VMEM,) * len(out_shape),
            scratch_shapes=[pltpu.VMEM((SN, SN), BF16)],
            compiler_params=params(6),
            cost_estimate=cost(2),
            name="prep",
        )(*operands)
        hold = []
        if group == 1:
            below.append(mask_below(1, packed))
            hold = below[1:]
        elif group > 1:
            more, kernel = (solved[:2], two_rows_kernel) if group == 2 else ([solved[2], sums, *anc_pieces], base_rows_kernel)
            sums = pl.pallas_call(
                kernel,
                out_shape=shape_of((below_rows, columns), F32),
                in_specs=[SMEM] + [VMEM] * (2 + len(more)),
                out_specs=VMEM,
                scratch_shapes=[pltpu.VMEM((below_rows, columns), BF16)] if last else [],
                input_output_aliases={4: 0} if last else {},
                compiler_params=params(6),
                cost_estimate=cost(3),
                name="rows_below",
            )(sn_order, *below, *more)
            hold = [sums]
        if group > 0:
            s = anc_order[group - 1]
            a_own, b_own, anc_pieces[s], *rest = lax.optimization_barrier((a_own, b_own, anc_pieces[s], *hold, *ready))
            hold, ready = rest[:len(hold)], rest[len(hold):]
            if group == 1:
                below[1:] = hold
            else:
                sums = hold[0]
        a_swap = swap(a_own, 1)
        b_swap = swap(b_own, 1)
        ready = list(ready) if last else list(ready) + [masked[group]]

        out_shape = [shape_of((PAIR, columns))]
        if not last:
            out_shape += [shape_of((SN, columns)), shape_of((half, columns))]
        results = pl.pallas_call(
            make_solve_kernel(group),
            out_shape=tuple(out_shape),
            in_specs=[SMEM] + [VMEM] * (5 + len(ready)),
            out_specs=(VMEM,) * len(out_shape),
            scratch_shapes=[pltpu.VMEM((PAIR, columns), BF16), pltpu.VMEM((2 * PAIR, columns), BF16)],
            compiler_params=params(8),
            cost_estimate=cost(3),
            name="pair_solve",
        )(tab, packed, a_own, a_swap, b_own, b_swap, *ready)
        solved.append(results[0])
        if not last:
            packed, part = results[1:]

    outputs = pl.pallas_call(
        last_rows_kernel,
        out_shape=(shape_of((NW, columns)), shape_of((below_rows, columns))),
        in_specs=[SMEM] + [VMEM] * 7,
        out_specs=(HBM, HBM),
        scratch_shapes=[pltpu.VMEM((below_rows, columns), BF16), pltpu.SemaphoreType.DMA((2 * GROUPS,)),
                        pltpu.SemaphoreType.DMA((4,))],
        compiler_params=params(6),
        cost_estimate=cost(3),
        name="last_rows",
    )(sn_order, *below, *solved, sums)

    def again(carry):
        carry, own_pieces, below_pieces = lax.optimization_barrier((carry, pieces, anc_pieces))
        back = carry[0][1] ^ jnp.arange(4)
        win_rhs = jnp.take(jnp.stack(own_pieces), back, axis=0).reshape(4 * tall, columns)
        anc_rhs = jnp.take(jnp.stack(below_pieces), back, axis=0).reshape(4 * tile, columns)
        return jnp.zeros_like(carry[0]), *general_path(
            win_rows, anc_rows, win_pattern, anc_pattern, window_owner, sn_order, diag_inv, win_rhs, anc_rhs)

    return tuple(lax.while_loop(lambda carry: carry[0][0] != 0, again, (flag, *outputs))[1:])


def solution(mesh):
    return jax.shard_map(
        local,
        mesh=mesh,
        in_specs=(P("rows", None), P("rows", None), P(), P("rows", None), P(), P(), P(),
                  P(("rows", "rhs"), None), P(("rows", "rhs"), None)),
        out_specs=(P(None, "rhs"), P("rows", "rhs")),
        check_vma=False,
    )
```

profile of v0, /device:TPU:0, one launch (start us, length us, event | category | flops | bytes accessed | tf_op | source)
XLA Modules:
  0.0 89.3 jit_solution(955351491860978539)
XLA Ops:
  0.7 2.4 %factor_pack.1.own_ref.refs_0_ = bf16[512,512]{1,0:T(8,128)(2,1)S(1)} custom-call(s32[64]{0:T(128)} %owner.4, s32[8]{0:T(128)} %order.21, s32[64,64]{1,0:T(8,128)} %pattern.8, bf16[512,4096]{1,0:T(8,128)(2,1)} %w_own.5), custom_call_target="tpu_custom_call" | custom-call | flops 200000000 | bytes 6000000 | tf_op jit(solution)/shard_map/factor_pack/pallas_call | solution.py:385
  3.6 1.5 %collective-permute-done.3.other_ref.refs_1_ = bf16[512,512]{1,0:T(8,128)(2,1)S(1)} collective-permute-done((bf16[512,512]{1,0:T(8,128)(2,1)S(1)}, bf16[512,512]{1,0:T(8,128)(2,1)S(1)}, u32[]{:S(2)}, u32[]{:S(2)}) %collective-permute-start.3) | collective-permute-done | bytes 524320 | tf_op jit(solution)/shard_map/ppermute | solution.py:357
  5.7 2.6 %collective-permute-start.14 = (bf16[1024,512]{1,0:T(8,128)(2,1)S(1)}, bf16[1024,512]{1,0:T(8,128)(2,1)S(1)}, u32[]{:S(2)}, u32[]{:S(2)}) collective-permute-start(bf16[1024,512]{1,0:T(8,128)(2,1)S(1)} %chip_pack.1), channel_id=1, source_target_pairs={{0,8},{4,20},{8,0},{12,28},{16,24},{20,4},{24,16},{28,12},{1,9},{5... | collective-permute-start | bytes 3145736 | tf_op jit(solution)/shard_map/ppermute | solution.py:363
  8.4 1.6 %collective-permute-start.5 = (bf16[128,256]{1,0:T(8,128)(2,1)S(1)}, bf16[128,256]{1,0:T(8,128)(2,1)S(1)}, u32[]{:S(2)}, u32[]{:S(2)}) collective-permute-start(bf16[128,256]{1,0:T(8,128)(2,1)S(1)} %get-tuple-element.377), channel_id=1, source_target_pairs={{0,1},{1,0},{2,3},{3,2},{4,5},{5,4},{6,7},{7,6},{8,9},{9,8},{10,11... | collective-permute-start | bytes 196616 | tf_op jit(solution)/shard_map/ppermute | solution.py:360
  10.0 2.6 %collective-permute-start.6 = (bf16[128,256]{1,0:T(8,128)(2,1)S(1)}, bf16[128,256]{1,0:T(8,128)(2,1)S(1)}, u32[]{:S(2)}, u32[]{:S(2)}) collective-permute-start(bf16[128,256]{1,0:T(8,128)(2,1)S(1)} %get-tuple-element.378), channel_id=1, source_target_pairs={{0,2},{1,3},{2,0},{3,1},{4,6},{5,7},{6,4},{7,5},{8,10},{9,11},{10,... | collective-permute-start | bytes 196616 | tf_op jit(solution)/shard_map/ppermute | solution.py:360
  12.8 3.6 %mask_below.2.a0 = bf16[1024,4096]{1,0:T(8,128)(2,1)S(1)} custom-call(s32[32,64]{1,0:T(8,128)S(1)} %copy-done.4, bf16[2048,4096]{1,0:T(8,128)(2,1)} %a_ref.3), custom_call_target="tpu_custom_call" | custom-call | flops 400000000 | bytes 12000000 | tf_op jit(solution)/shard_map/mask_below/pallas_call | solution.py:370
  17.5 1.2 %collective-permute-done.7.refs_3_ = bf16[128,256]{1,0:T(8,128)(2,1)S(1)} collective-permute-done((bf16[128,256]{1,0:T(8,128)(2,1)S(1)}, bf16[128,256]{1,0:T(8,128)(2,1)S(1)}, u32[]{:S(2)}, u32[]{:S(2)}) %collective-permute-start.7) | collective-permute-done | bytes 65568 | tf_op jit(solution)/shard_map/ppermute | solution.py:360
  21.4 1.8 %collective-permute-start.15 = (bf16[512,512]{1,0:T(8,128)(2,1)S(1)}, bf16[512,512]{1,0:T(8,128)(2,1)S(1)}, u32[]{:S(2)}, u32[]{:S(2)}) collective-permute-start(bf16[512,512]{1,0:T(8,128)(2,1)S(1)} %take_half.1), channel_id=1, source_target_pairs={{0,16},{4,12},{8,24},{12,4},{16,0},{20,28},{24,8},{28,20},{1,17},{... | collective-permute-start | bytes 1572872 | tf_op jit(solution)/shard_map/ppermute | solution.py:366
  23.2 1.5 %collective-permute-start.12 = (bf16[512,256]{1,0:T(8,128)(2,1)S(1)}, bf16[512,256]{1,0:T(8,128)(2,1)S(1)}, u32[]{:S(2)}, u32[]{:S(2)}) collective-permute-start(bf16[512,256]{1,0:T(8,128)(2,1)S(1)} %get-tuple-element.384.refs_1_), channel_id=1, source_target_pairs={{0,8},{4,20},{8,0},{12,28},{16,24},{20,4},{24,16},{28,12},{1,9},{5... | collective-permute-start | bytes 786440 | tf_op jit(solution)/shard_map/ppermute | solution.py:363
  25.0 1.9 %tables.1 = (s32[129]{0:T(256)S(1)}, s32[2]{0:T(128)}) custom-call(s32[64]{0:T(128)S(1)} %copy-done.20, s32[8]{0:T(128)S(1)} %copy-done.21), custom_call_target="tpu_custom_call" | custom-call | flops 200000000 | bytes 6000000 | tf_op jit(solution)/shard_map/tables/pallas_call | solution.py:445
  29.9 5.1 %collective-permute-done.13.refs_4_ = bf16[256,256]{1,0:T(8,128)(2,1)S(1)} collective-permute-done((bf16[256,256]{1,0:T(8,128)(2,1)S(1)}, bf16[256,256]{1,0:T(8,128)(2,1)S(1)}, u32[]{:S(2)}, u32[]{:S(2)}) %collective-permute-start.13) | collective-permute-done | bytes 131104 | tf_op jit(solution)/shard_map/ppermute | solution.py:357
  37.1 3.0 %collective-permute-start.22 = (bf16[512,256]{1,0:T(8,128)(2,1)S(1)}, bf16[512,256]{1,0:T(8,128)(2,1)S(1)}, u32[]{:S(2)}, u32[]{:S(2)}) collective-permute-start(bf16[512,256]{1,0:T(8,128)(2,1)S(1)} %get-tuple-element.405), channel_id=1, source_target_pairs={{0,2},{1,3},{2,0},{3,1},{4,6},{5,7},{6,4},{7,5},{8,10},{9,11},{10,... | collective-permute-start | bytes 786440 | tf_op jit(solution)/shard_map/ppermute | solution.py:360
  40.1 1.7 %prep.4 = (bf16[1024,1024]{1,0:T(8,128)(2,1)S(1)}, f32[512,256]{1,0:T(8,128)S(1)}) custom-call(s32[129]{0:T(256)S(1)} %get-tuple-element.389.tab.refs_0_, s32[8]{0:T(128)S(1)} %copy-done.21, bf16[8,512,512]{2,1,0:T(8,128)(2,1)S(1)} %copy-done.1, bf16[512,512]{1,0:T(8,128)(2,1)S(1)} %factor_pack.1.own_ref.refs_0_, ...), custom_call_target="tpu_custom_call" | custom-call | flops 200000000 | bytes 6000000 | tf_op jit(solution)/shard_map/prep/pallas_call | solution.py:504
  41.8 1.8 %pair_solve.4 = (bf16[1024,256]{1,0:T(8,128)(2,1)S(1)}, bf16[512,256]{1,0:T(8,128)(2,1)S(1)}, bf16[256,256]{1,0:T(8,128)(2,1)S(1)}) custom-call(s32[129]{0:T(256)S(1)} %get-tuple-element.389.tab.refs_0_, bf16[512,256]{1,0:T(8,128)(2,1)S(1)} %get-tuple-element.384.refs_1_, bf16[512,256]{1,0:T(8,128)(2,1)S(1)} %collective-permute-done.12.refs_2_, ...), custom_call_target="tpu_custom_call" | custom-call | flops 300000000 | bytes 9000000 | tf_op jit(solution)/shard_map/pair_solve/pallas_call | solution.py:547
  44.3 2.3 %collective-permute-start.21 = (bf16[256,256]{1,0:T(8,128)(2,1)S(1)}, bf16[256,256]{1,0:T(8,128)(2,1)S(1)}, u32[]{:S(2)}, u32[]{:S(2)}) collective-permute-start(bf16[256,256]{1,0:T(8,128)(2,1)S(1)} %get-tuple-element.402), channel_id=1, source_target_pairs={{0,24},{4,28},{8,16},{12,20},{16,8},{20,12},{24,0},{28,4},{1,25},{... | collective-permute-start | bytes 393224 | tf_op jit(solution)/shard_map/ppermute | solution.py:357
  46.7 2.3 %prep.5 = (bf16[1024,1024]{1,0:T(8,128)(2,1)S(1)}, f32[512,256]{1,0:T(8,128)S(1)}) custom-call(s32[129]{0:T(256)S(1)} %get-tuple-element.389.tab.refs_0_, s32[8]{0:T(128)S(1)} %copy-done.21, bf16[8,512,512]{2,1,0:T(8,128)(2,1)S(1)} %copy-done.1, bf16[512,512]{1,0:T(8,128)(2,1)S(1)} %factor_pack.1.own_ref.refs_0_, ...), custom_call_target="tpu_custom_call" | custom-call | flops 200000000 | bytes 6000000 | tf_op jit(solution)/shard_map/prep/pallas_call | solution.py:504
  49.0 3.6 %mask_below.3.a1 = bf16[1024,4096]{1,0:T(8,128)(2,1)S(1)} custom-call(s32[32,64]{1,0:T(8,128)S(1)} %copy-done.4, bf16[2048,4096]{1,0:T(8,128)(2,1)} %a_ref.3), custom_call_target="tpu_custom_call" | custom-call | flops 400000000 | bytes 12000000 | tf_op jit(solution)/shard_map/mask_below/pallas_call | solution.py:370
  52.6 1.2 %collective-permute-done.21.refs_4_ = bf16[256,256]{1,0:T(8,128)(2,1)S(1)} collective-permute-done((bf16[256,256]{1,0:T(8,128)(2,1)S(1)}, bf16[256,256]{1,0:T(8,128)(2,1)S(1)}, u32[]{:S(2)}, u32[]{:S(2)}) %collective-permute-start.21) | collective-permute-done | bytes 131104 | tf_op jit(solution)/shard_map/ppermute | solution.py:357
  54.3 3.2 %collective-permute-start.27 = (bf16[512,256]{1,0:T(8,128)(2,1)S(1)}, bf16[512,256]{1,0:T(8,128)(2,1)S(1)}, u32[]{:S(2)}, u32[]{:S(2)}) collective-permute-start(bf16[512,256]{1,0:T(8,128)(2,1)S(1)} %get-tuple-element.420), channel_id=1, source_target_pairs={{0,3},{1,2},{2,1},{3,0},{4,7},{5,6},{6,5},{7,4},{8,11},{9,10},{10,... | collective-permute-start | bytes 786440 | tf_op jit(solution)/shard_map/ppermute | solution.py:360
  57.5 1.8 %pair_solve.5 = (bf16[1024,256]{1,0:T(8,128)(2,1)S(1)}, bf16[512,256]{1,0:T(8,128)(2,1)S(1)}, bf16[256,256]{1,0:T(8,128)(2,1)S(1)}) custom-call(s32[129]{0:T(256)S(1)} %get-tuple-element.389.tab.refs_0_, bf16[512,256]{1,0:T(8,128)(2,1)S(1)} %get-tuple-element.401.refs_1_, bf16[512,256]{1,0:T(8,128)(2,1)S(1)} %collective-permute-done.20.refs_2_, ...), custom_call_target="tpu_custom_call" | custom-call | flops 300000000 | bytes 9000000 | tf_op jit(solution)/shard_map/pair_solve/pallas_call | solution.py:547
  59.9 1.4 %collective-permute-start.26 = (bf16[256,256]{1,0:T(8,128)(2,1)S(1)}, bf16[256,256]{1,0:T(8,128)(2,1)S(1)}, u32[]{:S(2)}, u32[]{:S(2)}) collective-permute-start(bf16[256,256]{1,0:T(8,128)(2,1)S(1)} %get-tuple-element.418), channel_id=1, source_target_pairs={{0,24},{4,28},{8,16},{12,20},{16,8},{20,12},{24,0},{28,4},{1,25},{... | collective-permute-start | bytes 393224 | tf_op jit(solution)/shard_map/ppermute | solution.py:357
  61.4 2.4 %prep.6 = (bf16[1024,1024]{1,0:T(8,128)(2,1)S(1)}, f32[512,256]{1,0:T(8,128)S(1)}) custom-call(s32[129]{0:T(256)S(1)} %get-tuple-element.389.tab.refs_0_, s32[8]{0:T(128)S(1)} %copy-done.21, bf16[8,512,512]{2,1,0:T(8,128)(2,1)S(1)} %copy-done.1, bf16[512,512]{1,0:T(8,128)(2,1)S(1)} %factor_pack.1.own_ref.refs_0_, ...), custom_call_target="tpu_custom_call" | custom-call | flops 200000000 | bytes 6000000 | tf_op jit(solution)/shard_map/prep/pallas_call | solution.py:504
  63.7 2.9 %rows_below.2.sums = f32[2048,256]{1,0:T(8,128)S(1)} custom-call(s32[8]{0:T(128)S(1)} %copy-done.21, bf16[1024,4096]{1,0:T(8,128)(2,1)S(1)} %mask_below.2.a0, bf16[1024,4096]{1,0:T(8,128)(2,1)S(1)} %mask_below.3.a1, bf16[1024,256]{1,0:T(8,128)(2,1)S(1)} %get-tuple-element.408.refs_8_.x0_ref.x0, bf16[1024,256]{1,0:T(8,128)(2,1)S(1)} %get-tuple-element.416.x1_ref.refs_9_.x1), custom_call_target="tpu_custom_call" | custom-call | flops 300000000 | bytes 9000000 | tf_op jit(solution)/shard_map/rows_below/pallas_call | solution.py:520
  66.6 1.8 %collective-permute-done.26.refs_4_ = bf16[256,256]{1,0:T(8,128)(2,1)S(1)} collective-permute-done((bf16[256,256]{1,0:T(8,128)(2,1)S(1)}, bf16[256,256]{1,0:T(8,128)(2,1)S(1)}, u32[]{:S(2)}, u32[]{:S(2)}) %collective-permute-start.26) | collective-permute-done | bytes 131104 | tf_op jit(solution)/shard_map/ppermute | solution.py:357
  69.0 1.2 %collective-permute-start.32 = (bf16[512,256]{1,0:T(8,128)(2,1)S(1)}, bf16[512,256]{1,0:T(8,128)(2,1)S(1)}, u32[]{:S(2)}, u32[]{:S(2)}) collective-permute-start(bf16[512,256]{1,0:T(8,128)(2,1)S(1)} %get-tuple-element.432), channel_id=1, source_target_pairs={{0,1},{1,0},{2,3},{3,2},{4,5},{5,4},{6,7},{7,6},{8,9},{9,8},{10,11... | collective-permute-start | bytes 786440 | tf_op jit(solution)/shard_map/ppermute | solution.py:360
  70.2 1.8 %pair_solve.6 = (bf16[1024,256]{1,0:T(8,128)(2,1)S(1)}, bf16[512,256]{1,0:T(8,128)(2,1)S(1)}, bf16[256,256]{1,0:T(8,128)(2,1)S(1)}) custom-call(s32[129]{0:T(256)S(1)} %get-tuple-element.389.tab.refs_0_, bf16[512,256]{1,0:T(8,128)(2,1)S(1)} %get-tuple-element.417.refs_1_, bf16[512,256]{1,0:T(8,128)(2,1)S(1)} %collective-permute-done.25.refs_2_, ...), custom_call_target="tpu_custom_call" | custom-call | flops 300000000 | bytes 9000000 | tf_op jit(solution)/shard_map/pair_solve/pallas_call | solution.py:547
  72.8 2.3 %collective-permute-start.31 = (bf16[256,256]{1,0:T(8,128)(2,1)S(1)}, bf16[256,256]{1,0:T(8,128)(2,1)S(1)}, u32[]{:S(2)}, u32[]{:S(2)}) collective-permute-start(bf16[256,256]{1,0:T(8,128)(2,1)S(1)} %get-tuple-element.430), channel_id=1, source_target_pairs={{0,24},{4,28},{8,16},{12,20},{16,8},{20,12},{24,0},{28,4},{1,25},{... | collective-permute-start | bytes 393224 | tf_op jit(solution)/shard_map/ppermute | solution.py:357
  75.1 1.7 %prep.7.refs_6_ = bf16[1024,1024]{1,0:T(8,128)(2,1)S(1)} custom-call(s32[129]{0:T(256)S(1)} %get-tuple-element.389.tab.refs_0_, s32[8]{0:T(128)S(1)} %copy-done.21, bf16[8,512,512]{2,1,0:T(8,128)(2,1)S(1)} %copy-done.1, bf16[512,512]{1,0:T(8,128)(2,1)S(1)} %factor_pack.1.own_ref.refs_0_, bf16[512,512]{1,0:T(8,128)(2,1)S(1)} %collective-permute-done.3.other_ref.refs_1_, ...), custom_call_target="tpu_custom_call" | custom-call | flops 200000000 | bytes 6000000 | tf_op jit(solution)/shard_map/prep/pallas_call | solution.py:504
  77.2 2.1 %rows_below.3.base = f32[2048,256]{1,0:T(8,128)S(1)} custom-call(s32[8]{0:T(128)S(1)} %copy-done.21, bf16[1024,4096]{1,0:T(8,128)(2,1)S(1)} %mask_below.2.a0, bf16[1024,4096]{1,0:T(8,128)(2,1)S(1)} %mask_below.3.a1, bf16[1024,256]{1,0:T(8,128)(2,1)S(1)} %get-tuple-element.428.x_ref.x2, ...), custom_call_target="tpu_custom_call", output_to_operand_aliasing={{}: (4, {})} | custom-call | flops 300000000 | bytes 9000000 | tf_op jit(solution)/shard_map/rows_below/pallas_call | solution.py:520
  79.3 2.9 %collective-permute-done.31.refs_4_ = bf16[256,256]{1,0:T(8,128)(2,1)S(1)} collective-permute-done((bf16[256,256]{1,0:T(8,128)(2,1)S(1)}, bf16[256,256]{1,0:T(8,128)(2,1)S(1)}, u32[]{:S(2)}, u32[]{:S(2)}) %collective-permute-start.31) | collective-permute-done | bytes 131104 | tf_op jit(solution)/shard_map/ppermute | solution.py:357
  82.7 1.2 %collective-permute-done.34.refs_5_ = bf16[256,256]{1,0:T(8,128)(2,1)S(1)} collective-permute-done((bf16[256,256]{1,0:T(8,128)(2,1)S(1)}, bf16[256,256]{1,0:T(8,128)(2,1)S(1)}, u32[]{:S(2)}, u32[]{:S(2)}) %collective-permute-start.34) | collective-permute-done | bytes 131104 | tf_op jit(solution)/shard_map/ppermute | solution.py:357
  85.1 3.0 %last_rows.1 = (bf16[4096,256]{1,0:T(8,128)(2,1)}, bf16[2048,256]{1,0:T(8,128)(2,1)}) custom-call(s32[8]{0:T(128)S(1)} %copy-done.21, bf16[1024,4096]{1,0:T(8,128)(2,1)S(1)} %mask_below.2.a0, bf16[1024,4096]{1,0:T(8,128)(2,1)S(1)} %mask_below.3.a1, bf16[1024,256]{1,0:T(8,128)(2,1)S(1)} %get-tuple-element.408.refs_8_.x0_ref.x0, ...), custom_call_target="tpu_custom_call" | custom-call | flops 300000000 | bytes 9000000 | tf_op jit(solution)/shard_map/last_rows/pallas_call | solution.py:561
  (72 shorter events, 16.6 us)
Async XLA Ops:
  3.1 2.1 %collective-permute-start.3 = (bf16[512,512]{1,0:T(8,128)(2,1)S(1)}, bf16[512,512]{1,0:T(8,128)(2,1)S(1)}, u32[]{:S(2)}, u32[]{:S(2)}) collective-permute-start(bf16[512,512]{1,0:T(8,128)(2,1)S(1)} %factor_pack.1.own_ref.refs_0_), channel_id=1, source_target_pairs={{0,4},{4,0},{8,12},{12,8},{16,20},{20,16},{24,28},{28,24},{1,5},{5... | collective-permute-start | bytes 1572872 | tf_op jit(solution)/shard_map/ppermute | solution.py:357
  5.3 13.5 %collective-permute-start.4 = (bf16[512,4096]{1,0:T(8,128)(2,1)S(1)}, bf16[512,4096]{1,0:T(8,128)(2,1)S(1)}, u32[]{:S(2)}, u32[]{:S(2)}) collective-permute-start(bf16[512,4096]{1,0:T(8,128)(2,1)S(1)} %copy-done), channel_id=1, source_target_pairs={{0,4},{4,0},{8,12},{12,8},{16,20},{20,16},{24,28},{28,24},{1,5},{5... | collective-permute-start | bytes 12582920 | tf_op jit(solution)/shard_map/ppermute | solution.py:357
  5.7 15.7 %collective-permute-start.14 = (bf16[1024,512]{1,0:T(8,128)(2,1)S(1)}, bf16[1024,512]{1,0:T(8,128)(2,1)S(1)}, u32[]{:S(2)}, u32[]{:S(2)}) collective-permute-start(bf16[1024,512]{1,0:T(8,128)(2,1)S(1)} %chip_pack.1), channel_id=1, source_target_pairs={{0,8},{4,20},{8,0},{12,28},{16,24},{20,4},{24,16},{28,12},{1,9},{5... | collective-permute-start | bytes 3145736 | tf_op jit(solution)/shard_map/ppermute | solution.py:363
  8.4 8.0 %collective-permute-start.5 = (bf16[128,256]{1,0:T(8,128)(2,1)S(1)}, bf16[128,256]{1,0:T(8,128)(2,1)S(1)}, u32[]{:S(2)}, u32[]{:S(2)}) collective-permute-start(bf16[128,256]{1,0:T(8,128)(2,1)S(1)} %get-tuple-element.377), channel_id=1, source_target_pairs={{0,1},{1,0},{2,3},{3,2},{4,5},{5,4},{6,7},{7,6},{8,9},{9,8},{10,11... | collective-permute-start | bytes 196616 | tf_op jit(solution)/shard_map/ppermute | solution.py:360
  10.0 7.5 %collective-permute-start.6 = (bf16[128,256]{1,0:T(8,128)(2,1)S(1)}, bf16[128,256]{1,0:T(8,128)(2,1)S(1)}, u32[]{:S(2)}, u32[]{:S(2)}) collective-permute-start(bf16[128,256]{1,0:T(8,128)(2,1)S(1)} %get-tuple-element.378), channel_id=1, source_target_pairs={{0,2},{1,3},{2,0},{3,1},{4,6},{5,7},{6,4},{7,5},{8,10},{9,11},{10,... | collective-permute-start | bytes 196616 | tf_op jit(solution)/shard_map/ppermute | solution.py:360
  12.6 6.2 %collective-permute-start.7 = (bf16[128,256]{1,0:T(8,128)(2,1)S(1)}, bf16[128,256]{1,0:T(8,128)(2,1)S(1)}, u32[]{:S(2)}, u32[]{:S(2)}) collective-permute-start(bf16[128,256]{1,0:T(8,128)(2,1)S(1)} %get-tuple-element.379), channel_id=1, source_target_pairs={{0,3},{1,2},{2,1},{3,0},{4,7},{5,6},{6,5},{7,4},{8,11},{9,10},{10,... | collective-permute-start | bytes 196616 | tf_op jit(solution)/shard_map/ppermute | solution.py:360
  18.8 1.3 %collective-permute-start.8 = (bf16[128,256]{1,0:T(8,128)(2,1)S(1)}, bf16[128,256]{1,0:T(8,128)(2,1)S(1)}, u32[]{:S(2)}, u32[]{:S(2)}) collective-permute-start(bf16[128,256]{1,0:T(8,128)(2,1)S(1)} %get-tuple-element.803.refs_0_), channel_id=1, source_target_pairs={{0,4},{4,0},{8,12},{12,8},{16,20},{20,16},{24,28},{28,24},{1,5},{5... | collective-permute-start | bytes 196616 | tf_op jit(solution)/shard_map/ppermute | solution.py:357
  18.8 1.4 %collective-permute-start.9 = (bf16[128,256]{1,0:T(8,128)(2,1)S(1)}, bf16[128,256]{1,0:T(8,128)(2,1)S(1)}, u32[]{:S(2)}, u32[]{:S(2)}) collective-permute-start(bf16[128,256]{1,0:T(8,128)(2,1)S(1)} %collective-permute-done.5.refs_1_), channel_id=1, source_target_pairs={{0,4},{4,0},{8,12},{12,8},{16,20},{20,16},{24,28},{28,24},{1,5},{5... | collective-permute-start | bytes 196616 | tf_op jit(solution)/shard_map/ppermute | solution.py:357
  19.3 1.3 %collective-permute-start.10 = (bf16[128,256]{1,0:T(8,128)(2,1)S(1)}, bf16[128,256]{1,0:T(8,128)(2,1)S(1)}, u32[]{:S(2)}, u32[]{:S(2)}) collective-permute-start(bf16[128,256]{1,0:T(8,128)(2,1)S(1)} %collective-permute-done.6.refs_2_), channel_id=1, source_target_pairs={{0,4},{4,0},{8,12},{12,8},{16,20},{20,16},{24,28},{28,24},{1,5},{5... | collective-permute-start | bytes 196616 | tf_op jit(solution)/shard_map/ppermute | solution.py:357
  19.3 1.4 %collective-permute-start.11 = (bf16[128,256]{1,0:T(8,128)(2,1)S(1)}, bf16[128,256]{1,0:T(8,128)(2,1)S(1)}, u32[]{:S(2)}, u32[]{:S(2)}) collective-permute-start(bf16[128,256]{1,0:T(8,128)(2,1)S(1)} %collective-permute-done.7.refs_3_), channel_id=1, source_target_pairs={{0,4},{4,0},{8,12},{12,8},{16,20},{20,16},{24,28},{28,24},{1,5},{5... | collective-permute-start | bytes 196616 | tf_op jit(solution)/shard_map/ppermute | solution.py:357
  21.4 13.9 %collective-permute-start.15 = (bf16[512,512]{1,0:T(8,128)(2,1)S(1)}, bf16[512,512]{1,0:T(8,128)(2,1)S(1)}, u32[]{:S(2)}, u32[]{:S(2)}) collective-permute-start(bf16[512,512]{1,0:T(8,128)(2,1)S(1)} %take_half.1), channel_id=1, source_target_pairs={{0,16},{4,12},{8,24},{12,4},{16,0},{20,28},{24,8},{28,20},{1,17},{... | collective-permute-start | bytes 1572872 | tf_op jit(solution)/shard_map/ppermute | solution.py:366
  23.2 11.7 %collective-permute-start.12 = (bf16[512,256]{1,0:T(8,128)(2,1)S(1)}, bf16[512,256]{1,0:T(8,128)(2,1)S(1)}, u32[]{:S(2)}, u32[]{:S(2)}) collective-permute-start(bf16[512,256]{1,0:T(8,128)(2,1)S(1)} %get-tuple-element.384.refs_1_), channel_id=1, source_target_pairs={{0,8},{4,20},{8,0},{12,28},{16,24},{20,4},{24,16},{28,12},{1,9},{5... | collective-permute-start | bytes 786440 | tf_op jit(solution)/shard_map/ppermute | solution.py:363
  24.7 10.2 %collective-permute-start.13 = (bf16[256,256]{1,0:T(8,128)(2,1)S(1)}, bf16[256,256]{1,0:T(8,128)(2,1)S(1)}, u32[]{:S(2)}, u32[]{:S(2)}) collective-permute-start(bf16[256,256]{1,0:T(8,128)(2,1)S(1)} %get-tuple-element.390), channel_id=1, source_target_pairs={{0,24},{4,28},{8,16},{12,20},{16,8},{20,12},{24,0},{28,4},{1,25},{... | collective-permute-start | bytes 393224 | tf_op jit(solution)/shard_map/ppermute | solution.py:357
  35.4 4.8 %collective-permute-start.18 = (bf16[1024,512]{1,0:T(8,128)(2,1)S(1)}, bf16[1024,512]{1,0:T(8,128)(2,1)S(1)}, u32[]{:S(2)}, u32[]{:S(2)}) collective-permute-start(bf16[1024,512]{1,0:T(8,128)(2,1)S(1)} %collective-permute-done.14.x_ref.refs_2_), channel_id=1, source_target_pairs={{0,4},{4,0},{8,12},{12,8},{16,20},{20,16},{24,28},{28,24},{1,5},{5... | collective-permute-start | bytes 3145736 | tf_op jit(solution)/shard_map/ppermute | solution.py:357
  36.4 3.7 %collective-permute-start.19 = (bf16[512,512]{1,0:T(8,128)(2,1)S(1)}, bf16[512,512]{1,0:T(8,128)(2,1)S(1)}, u32[]{:S(2)}, u32[]{:S(2)}) collective-permute-start(bf16[512,512]{1,0:T(8,128)(2,1)S(1)} %collective-permute-done.15.refs_4_), channel_id=1, source_target_pairs={{0,4},{4,0},{8,12},{12,8},{16,20},{20,16},{24,28},{28,24},{1,5},{5... | collective-permute-start | bytes 1572872 | tf_op jit(solution)/shard_map/ppermute | solution.py:357
  36.4 5.4 %collective-permute-start.16 = (bf16[512,256]{1,0:T(8,128)(2,1)S(1)}, bf16[512,256]{1,0:T(8,128)(2,1)S(1)}, u32[]{:S(2)}, u32[]{:S(2)}) collective-permute-start(bf16[512,256]{1,0:T(8,128)(2,1)S(1)} %collective-permute-done.12.refs_2_), channel_id=1, source_target_pairs={{0,4},{4,0},{8,12},{12,8},{16,20},{20,16},{24,28},{28,24},{1,5},{5... | collective-permute-start | bytes 786440 | tf_op jit(solution)/shard_map/ppermute | solution.py:357
  36.9 4.9 %collective-permute-start.17 = (bf16[256,256]{1,0:T(8,128)(2,1)S(1)}, bf16[256,256]{1,0:T(8,128)(2,1)S(1)}, u32[]{:S(2)}, u32[]{:S(2)}) collective-permute-start(bf16[256,256]{1,0:T(8,128)(2,1)S(1)} %collective-permute-done.13.refs_4_), channel_id=1, source_target_pairs={{0,4},{4,0},{8,12},{12,8},{16,20},{20,16},{24,28},{28,24},{1,5},{5... | collective-permute-start | bytes 393224 | tf_op jit(solution)/shard_map/ppermute | solution.py:357
  37.1 15.5 %collective-permute-start.22 = (bf16[512,256]{1,0:T(8,128)(2,1)S(1)}, bf16[512,256]{1,0:T(8,128)(2,1)S(1)}, u32[]{:S(2)}, u32[]{:S(2)}) collective-permute-start(bf16[512,256]{1,0:T(8,128)(2,1)S(1)} %get-tuple-element.405), channel_id=1, source_target_pairs={{0,2},{1,3},{2,0},{3,1},{4,6},{5,7},{6,4},{7,5},{8,10},{9,11},{10,... | collective-permute-start | bytes 786440 | tf_op jit(solution)/shard_map/ppermute | solution.py:360
  43.6 10.2 %collective-permute-start.20 = (bf16[512,256]{1,0:T(8,128)(2,1)S(1)}, bf16[512,256]{1,0:T(8,128)(2,1)S(1)}, u32[]{:S(2)}, u32[]{:S(2)}) collective-permute-start(bf16[512,256]{1,0:T(8,128)(2,1)S(1)} %get-tuple-element.401.refs_1_), channel_id=1, source_target_pairs={{0,8},{4,20},{8,0},{12,28},{16,24},{20,4},{24,16},{28,12},{1,9},{5... | collective-permute-start | bytes 786440 | tf_op jit(solution)/shard_map/ppermute | solution.py:363
  44.3 9.5 %collective-permute-start.21 = (bf16[256,256]{1,0:T(8,128)(2,1)S(1)}, bf16[256,256]{1,0:T(8,128)(2,1)S(1)}, u32[]{:S(2)}, u32[]{:S(2)}) collective-permute-start(bf16[256,256]{1,0:T(8,128)(2,1)S(1)} %get-tuple-element.402), channel_id=1, source_target_pairs={{0,24},{4,28},{8,16},{12,20},{16,8},{20,12},{24,0},{28,4},{1,25},{... | collective-permute-start | bytes 393224 | tf_op jit(solution)/shard_map/ppermute | solution.py:357
  53.8 3.7 %collective-permute-start.23 = (bf16[512,256]{1,0:T(8,128)(2,1)S(1)}, bf16[512,256]{1,0:T(8,128)(2,1)S(1)}, u32[]{:S(2)}, u32[]{:S(2)}) collective-permute-start(bf16[512,256]{1,0:T(8,128)(2,1)S(1)} %collective-permute-done.20.refs_2_), channel_id=1, source_target_pairs={{0,4},{4,0},{8,12},{12,8},{16,20},{20,16},{24,28},{28,24},{1,5},{5... | collective-permute-start | bytes 786440 | tf_op jit(solution)/shard_map/ppermute | solution.py:357
  53.8 3.7 %collective-permute-start.24 = (bf16[256,256]{1,0:T(8,128)(2,1)S(1)}, bf16[256,256]{1,0:T(8,128)(2,1)S(1)}, u32[]{:S(2)}, u32[]{:S(2)}) collective-permute-start(bf16[256,256]{1,0:T(8,128)(2,1)S(1)} %collective-permute-done.21.refs_4_), channel_id=1, source_target_pairs={{0,4},{4,0},{8,12},{12,8},{16,20},{20,16},{24,28},{28,24},{1,5},{5... | collective-permute-start | bytes 393224 | tf_op jit(solution)/shard_map/ppermute | solution.py:357
  54.3 12.3 %collective-permute-start.27 = (bf16[512,256]{1,0:T(8,128)(2,1)S(1)}, bf16[512,256]{1,0:T(8,128)(2,1)S(1)}, u32[]{:S(2)}, u32[]{:S(2)}) collective-permute-start(bf16[512,256]{1,0:T(8,128)(2,1)S(1)} %get-tuple-element.420), channel_id=1, source_target_pairs={{0,3},{1,2},{2,1},{3,0},{4,7},{5,6},{6,5},{7,4},{8,11},{9,10},{10,... | collective-permute-start | bytes 786440 | tf_op jit(solution)/shard_map/ppermute | solution.py:360
  59.3 9.1 %collective-permute-start.25 = (bf16[512,256]{1,0:T(8,128)(2,1)S(1)}, bf16[512,256]{1,0:T(8,128)(2,1)S(1)}, u32[]{:S(2)}, u32[]{:S(2)}) collective-permute-start(bf16[512,256]{1,0:T(8,128)(2,1)S(1)} %get-tuple-element.417.refs_1_), channel_id=1, source_target_pairs={{0,8},{4,20},{8,0},{12,28},{16,24},{20,4},{24,16},{28,12},{1,9},{5... | collective-permute-start | bytes 786440 | tf_op jit(solution)/shard_map/ppermute | solution.py:363
  59.9 8.5 %collective-permute-start.26 = (bf16[256,256]{1,0:T(8,128)(2,1)S(1)}, bf16[256,256]{1,0:T(8,128)(2,1)S(1)}, u32[]{:S(2)}, u32[]{:S(2)}) collective-permute-start(bf16[256,256]{1,0:T(8,128)(2,1)S(1)} %get-tuple-element.418), channel_id=1, source_target_pairs={{0,24},{4,28},{8,16},{12,20},{16,8},{20,12},{24,0},{28,4},{1,25},{... | collective-permute-start | bytes 393224 | tf_op jit(solution)/shard_map/ppermute | solution.py:357
  68.5 1.8 %collective-permute-start.28 = (bf16[512,256]{1,0:T(8,128)(2,1)S(1)}, bf16[512,256]{1,0:T(8,128)(2,1)S(1)}, u32[]{:S(2)}, u32[]{:S(2)}) collective-permute-start(bf16[512,256]{1,0:T(8,128)(2,1)S(1)} %collective-permute-done.25.refs_2_), channel_id=1, source_target_pairs={{0,4},{4,0},{8,12},{12,8},{16,20},{20,16},{24,28},{28,24},{1,5},{5... | collective-permute-start | bytes 786440 | tf_op jit(solution)/shard_map/ppermute | solution.py:357
  68.5 1.7 %collective-permute-start.29 = (bf16[256,256]{1,0:T(8,128)(2,1)S(1)}, bf16[256,256]{1,0:T(8,128)(2,1)S(1)}, u32[]{:S(2)}, u32[]{:S(2)}) collective-permute-start(bf16[256,256]{1,0:T(8,128)(2,1)S(1)} %collective-permute-done.26.refs_4_), channel_id=1, source_target_pairs={{0,4},{4,0},{8,12},{12,8},{16,20},{20,16},{24,28},{28,24},{1,5},{5... | collective-permute-start | bytes 393224 | tf_op jit(solution)/shard_map/ppermute | solution.py:357
  69.0 8.2 %collective-permute-start.32 = (bf16[512,256]{1,0:T(8,128)(2,1)S(1)}, bf16[512,256]{1,0:T(8,128)(2,1)S(1)}, u32[]{:S(2)}, u32[]{:S(2)}) collective-permute-start(bf16[512,256]{1,0:T(8,128)(2,1)S(1)} %get-tuple-element.432), channel_id=1, source_target_pairs={{0,1},{1,0},{2,3},{3,2},{4,5},{5,4},{6,7},{7,6},{8,9},{9,8},{10,11... | collective-permute-start | bytes 786440 | tf_op jit(solution)/shard_map/ppermute | solution.py:360
  72.0 10.2 %collective-permute-start.30 = (bf16[512,256]{1,0:T(8,128)(2,1)S(1)}, bf16[512,256]{1,0:T(8,128)(2,1)S(1)}, u32[]{:S(2)}, u32[]{:S(2)}) collective-permute-start(bf16[512,256]{1,0:T(8,128)(2,1)S(1)} %get-tuple-element.429.refs_1_), channel_id=1, source_target_pairs={{0,8},{4,20},{8,0},{12,28},{16,24},{20,4},{24,16},{28,12},{1,9},{5... | collective-permute-start | bytes 786440 | tf_op jit(solution)/shard_map/ppermute | solution.py:363
  72.8 9.4 %collective-permute-start.31 = (bf16[256,256]{1,0:T(8,128)(2,1)S(1)}, bf16[256,256]{1,0:T(8,128)(2,1)S(1)}, u32[]{:S(2)}, u32[]{:S(2)}) collective-permute-start(bf16[256,256]{1,0:T(8,128)(2,1)S(1)} %get-tuple-element.430), channel_id=1, source_target_pairs={{0,24},{4,28},{8,16},{12,20},{16,8},{20,12},{24,0},{28,4},{1,25},{... | collective-permute-start | bytes 393224 | tf_op jit(solution)/shard_map/ppermute | solution.py:357
  82.2 1.7 %collective-permute-start.33 = (bf16[512,256]{1,0:T(8,128)(2,1)S(1)}, bf16[512,256]{1,0:T(8,128)(2,1)S(1)}, u32[]{:S(2)}, u32[]{:S(2)}) collective-permute-start(bf16[512,256]{1,0:T(8,128)(2,1)S(1)} %collective-permute-done.30.refs_2_), channel_id=1, source_target_pairs={{0,4},{4,0},{8,12},{12,8},{16,20},{20,16},{24,28},{28,24},{1,5},{5... | collective-permute-start | bytes 786440 | tf_op jit(solution)/shard_map/ppermute | solution.py:357
  82.2 1.7 %collective-permute-start.34 = (bf16[256,256]{1,0:T(8,128)(2,1)S(1)}, bf16[256,256]{1,0:T(8,128)(2,1)S(1)}, u32[]{:S(2)}, u32[]{:S(2)}) collective-permute-start(bf16[256,256]{1,0:T(8,128)(2,1)S(1)} %collective-permute-done.31.refs_4_), channel_id=1, source_target_pairs={{0,4},{4,0},{8,12},{12,8},{16,20},{20,16},{24,28},{28,24},{1,5},{5... | collective-permute-start | bytes 393224 | tf_op jit(solution)/shard_map/ppermute | solution.py:357
  (8 other events, 68.2 us)
where the time goes:
time: 89.4 us; the launch traced here: 89.3 us
  Pallas kernels  38 us (43%)
  starting transfers between devices  31.3 us (35%)
  waiting for transfers between devices  17.9 us (20%)
  between operations  1.12 us (1%)
  loops' own time  0.9 us (1%)
    ppermute x20, waiting for transfers between devices, swap(): return lax.ppermute(x, 'rows', [(i, i ^ m) for i in range(8)])  14.7 us
    ppermute x6, starting transfers between devices, deep(): return lax.ppermute(x, 'rhs', [(i, i ^ m) for i in range(4)])  11.9 us
    ppermute x20, starting transfers between devices, swap(): return lax.ppermute(x, 'rows', [(i, i ^ m) for i in range(8)])  11.4 us
    pallas_call x4, Pallas kernels, local(): pl.pallas_call(make_prep_kernel(group), out_shape=tuple(out_shape), in_sp...  8 us
    pallas_call x2, Pallas kernels, mask_below(): pl.pallas_call(make_below_mask_kernel(k), out_shape=shape_of((PAIR, NW)),...  7.11 us
    pallas_call x4, Pallas kernels, local(): pl.pallas_call(make_solve_kernel(group), out_shape=tuple(out_shape), in_s...  6.59 us
    ppermute x5, starting transfers between devices, neighbour(): lax.ppermute(x, 'rows', [(i, i ^ (2 if i % 2 == 0 else 4)) for i in range...  6.15 us
    pallas_call x2, Pallas kernels, local(): pl.pallas_call(kernel, out_shape=shape_of((below_rows, columns), F32), in...  5 us
  transfers between devices with their start and end apart: 32, of which 14 were waited for; matrix products, arithmetic and copies ran while one was open for 0% of the time, Pallas kernels for 35%

commit v1 on v0

--- a/solution.py
+++ b/solution.py
@@ -459,7 +459,7 @@
     diag_vmem = in_vmem(diag_inv)
     below_rows = anc_rows.shape[0]
 
-    anc_order, anc_pieces = (2, 3, 1), [None] * 4
+    anc_order, anc_pieces = (2, 1, 3), [None] * 4
     for group in range(GROUPS):
         last = group == GROUPS - 1
         a_own = neighbour(packed)

time: 89.4 us -> 89.4 us (level)
  no operation moved by 1% of the time
where the time goes in v1:
time: 89.4 us; the launch traced here: 89.3 us
  Pallas kernels  38 us (43%)
  starting transfers between devices  31.3 us (35%)
  waiting for transfers between devices  17.9 us (20%)
  between operations  1.12 us (1%)
  loops' own time  0.9 us (1%)
    ppermute x20, waiting for transfers between devices, swap(): return lax.ppermute(x, 'rows', [(i, i ^ m) for i in range(8)])  14.4 us
    ppermute x6, starting transfers between devices, deep(): return lax.ppermute(x, 'rhs', [(i, i ^ m) for i in range(4)])  11.9 us
    ppermute x20, starting transfers between devices, swap(): return lax.ppermute(x, 'rows', [(i, i ^ m) for i in range(8)])  11.4 us
    pallas_call x4, Pallas kernels, local(): pl.pallas_call(make_prep_kernel(group), out_shape=tuple(out_shape), in_sp...  8 us
    pallas_call x2, Pallas kernels, mask_below(): pl.pallas_call(make_below_mask_kernel(k), out_shape=shape_of((PAIR, NW)),...  7.11 us
    pallas_call x4, Pallas kernels, local(): pl.pallas_call(make_solve_kernel(group), out_shape=tuple(out_shape), in_s...  6.59 us
    ppermute x5, starting transfers between devices, neighbour(): lax.ppermute(x, 'rows', [(i, i ^ (2 if i % 2 == 0 else 4)) for i in range...  6.16 us
    pallas_call x2, Pallas kernels, local(): pl.pallas_call(kernel, out_shape=shape_of((below_rows, columns), F32), in...  5 us
  transfers between devices with their start and end apart: 32, of which 14 were waited for; matrix products, arithmetic and copies ran while one was open for 0% of the time, Pallas kernels for 35%

profile of v1, /device:TPU:0, one launch (start us, length us, event | category | flops | bytes accessed | tf_op | source)
XLA Modules:
  0.0 89.3 jit_solution(2080815251868031795)
XLA Ops:
  0.7 2.4 %factor_pack.1.own_ref.refs_0_ = bf16[512,512]{1,0:T(8,128)(2,1)S(1)} custom-call(s32[64]{0:T(128)} %owner.4, s32[8]{0:T(128)} %order.21, s32[64,64]{1,0:T(8,128)} %pattern.8, bf16[512,4096]{1,0:T(8,128)(2,1)} %w_own.5), custom_call_target="tpu_custom_call" | custom-call | flops 200000000 | bytes 6000000 | tf_op jit(solution)/shard_map/factor_pack/pallas_call | solution.py:385
  3.6 1.5 %collective-permute-done.3.other_ref.refs_1_ = bf16[512,512]{1,0:T(8,128)(2,1)S(1)} collective-permute-done((bf16[512,512]{1,0:T(8,128)(2,1)S(1)}, bf16[512,512]{1,0:T(8,128)(2,1)S(1)}, u32[]{:S(2)}, u32[]{:S(2)}) %collective-permute-start.3) | collective-permute-done | bytes 524320 | tf_op jit(solution)/shard_map/ppermute | solution.py:357
  5.7 2.6 %collective-permute-start.14 = (bf16[1024,512]{1,0:T(8,128)(2,1)S(1)}, bf16[1024,512]{1,0:T(8,128)(2,1)S(1)}, u32[]{:S(2)}, u32[]{:S(2)}) collective-permute-start(bf16[1024,512]{1,0:T(8,128)(2,1)S(1)} %chip_pack.1), channel_id=1, source_target_pairs={{0,8},{4,20},{8,0},{12,28},{16,24},{20,4},{24,16},{28,12},{1,9},{5... | collective-permute-start | bytes 3145736 | tf_op jit(solution)/shard_map/ppermute | solution.py:363
  8.4 1.6 %collective-permute-start.5 = (bf16[128,256]{1,0:T(8,128)(2,1)S(1)}, bf16[128,256]{1,0:T(8,128)(2,1)S(1)}, u32[]{:S(2)}, u32[]{:S(2)}) collective-permute-start(bf16[128,256]{1,0:T(8,128)(2,1)S(1)} %get-tuple-element.377), channel_id=1, source_target_pairs={{0,1},{1,0},{2,3},{3,2},{4,5},{5,4},{6,7},{7,6},{8,9},{9,8},{10,11... | collective-permute-start | bytes 196616 | tf_op jit(solution)/shard_map/ppermute | solution.py:360
  10.0 2.6 %collective-permute-start.6 = (bf16[128,256]{1,0:T(8,128)(2,1)S(1)}, bf16[128,256]{1,0:T(8,128)(2,1)S(1)}, u32[]{:S(2)}, u32[]{:S(2)}) collective-permute-start(bf16[128,256]{1,0:T(8,128)(2,1)S(1)} %get-tuple-element.378), channel_id=1, source_target_pairs={{0,2},{1,3},{2,0},{3,1},{4,6},{5,7},{6,4},{7,5},{8,10},{9,11},{10,... | collective-permute-start | bytes 196616 | tf_op jit(solution)/shard_map/ppermute | solution.py:360
  12.8 3.6 %mask_below.2.a0 = bf16[1024,4096]{1,0:T(8,128)(2,1)S(1)} custom-call(s32[32,64]{1,0:T(8,128)S(1)} %copy-done.4, bf16[2048,4096]{1,0:T(8,128)(2,1)} %a_ref.3), custom_call_target="tpu_custom_call" | custom-call | flops 400000000 | bytes 12000000 | tf_op jit(solution)/shard_map/mask_below/pallas_call | solution.py:370
  17.5 1.2 %collective-permute-done.7.refs_3_ = bf16[128,256]{1,0:T(8,128)(2,1)S(1)} collective-permute-done((bf16[128,256]{1,0:T(8,128)(2,1)S(1)}, bf16[128,256]{1,0:T(8,128)(2,1)S(1)}, u32[]{:S(2)}, u32[]{:S(2)}) %collective-permute-start.7) | collective-permute-done | bytes 65568 | tf_op jit(solution)/shard_map/ppermute | solution.py:360
  21.4 1.8 %collective-permute-start.15 = (bf16[512,512]{1,0:T(8,128)(2,1)S(1)}, bf16[512,512]{1,0:T(8,128)(2,1)S(1)}, u32[]{:S(2)}, u32[]{:S(2)}) collective-permute-start(bf16[512,512]{1,0:T(8,128)(2,1)S(1)} %take_half.1), channel_id=1, source_target_pairs={{0,16},{4,12},{8,24},{12,4},{16,0},{20,28},{24,8},{28,20},{1,17},{... | collective-permute-start | bytes 1572872 | tf_op jit(solution)/shard_map/ppermute | solution.py:366
  23.2 1.5 %collective-permute-start.12 = (bf16[512,256]{1,0:T(8,128)(2,1)S(1)}, bf16[512,256]{1,0:T(8,128)(2,1)S(1)}, u32[]{:S(2)}, u32[]{:S(2)}) collective-permute-start(bf16[512,256]{1,0:T(8,128)(2,1)S(1)} %get-tuple-element.384.refs_1_), channel_id=1, source_target_pairs={{0,8},{4,20},{8,0},{12,28},{16,24},{20,4},{24,16},{28,12},{1,9},{5... | collective-permute-start | bytes 786440 | tf_op jit(solution)/shard_map/ppermute | solution.py:363
  25.0 1.9 %tables.1 = (s32[129]{0:T(256)S(1)}, s32[2]{0:T(128)}) custom-call(s32[64]{0:T(128)S(1)} %copy-done.20, s32[8]{0:T(128)S(1)} %copy-done.21), custom_call_target="tpu_custom_call" | custom-call | flops 200000000 | bytes 6000000 | tf_op jit(solution)/shard_map/tables/pallas_call | solution.py:445
  29.9 5.1 %collective-permute-done.13.refs_4_ = bf16[256,256]{1,0:T(8,128)(2,1)S(1)} collective-permute-done((bf16[256,256]{1,0:T(8,128)(2,1)S(1)}, bf16[256,256]{1,0:T(8,128)(2,1)S(1)}, u32[]{:S(2)}, u32[]{:S(2)}) %collective-permute-start.13) | collective-permute-done | bytes 131104 | tf_op jit(solution)/shard_map/ppermute | solution.py:357
  37.1 3.0 %collective-permute-start.22 = (bf16[512,256]{1,0:T(8,128)(2,1)S(1)}, bf16[512,256]{1,0:T(8,128)(2,1)S(1)}, u32[]{:S(2)}, u32[]{:S(2)}) collective-permute-start(bf16[512,256]{1,0:T(8,128)(2,1)S(1)} %get-tuple-element.405), channel_id=1, source_target_pairs={{0,2},{1,3},{2,0},{3,1},{4,6},{5,7},{6,4},{7,5},{8,10},{9,11},{10,... | collective-permute-start | bytes 786440 | tf_op jit(solution)/shard_map/ppermute | solution.py:360
  40.1 1.7 %prep.4 = (bf16[1024,1024]{1,0:T(8,128)(2,1)S(1)}, f32[512,256]{1,0:T(8,128)S(1)}) custom-call(s32[129]{0:T(256)S(1)} %get-tuple-element.389.tab.refs_0_, s32[8]{0:T(128)S(1)} %copy-done.21, bf16[8,512,512]{2,1,0:T(8,128)(2,1)S(1)} %copy-done.1, bf16[512,512]{1,0:T(8,128)(2,1)S(1)} %factor_pack.1.own_ref.refs_0_, ...), custom_call_target="tpu_custom_call" | custom-call | flops 200000000 | bytes 6000000 | tf_op jit(solution)/shard_map/prep/pallas_call | solution.py:504
  41.8 1.8 %pair_solve.4 = (bf16[1024,256]{1,0:T(8,128)(2,1)S(1)}, bf16[512,256]{1,0:T(8,128)(2,1)S(1)}, bf16[256,256]{1,0:T(8,128)(2,1)S(1)}) custom-call(s32[129]{0:T(256)S(1)} %get-tuple-element.389.tab.refs_0_, bf16[512,256]{1,0:T(8,128)(2,1)S(1)} %get-tuple-element.384.refs_1_, bf16[512,256]{1,0:T(8,128)(2,1)S(1)} %collective-permute-done.12.refs_2_, ...), custom_call_target="tpu_custom_call" | custom-call | flops 300000000 | bytes 9000000 | tf_op jit(solution)/shard_map/pair_solve/pallas_call | solution.py:547
  44.3 2.3 %collective-permute-start.21 = (bf16[256,256]{1,0:T(8,128)(2,1)S(1)}, bf16[256,256]{1,0:T(8,128)(2,1)S(1)}, u32[]{:S(2)}, u32[]{:S(2)}) collective-permute-start(bf16[256,256]{1,0:T(8,128)(2,1)S(1)} %get-tuple-element.402), channel_id=1, source_target_pairs={{0,24},{4,28},{8,16},{12,20},{16,8},{20,12},{24,0},{28,4},{1,25},{... | collective-permute-start | bytes 393224 | tf_op jit(solution)/shard_map/ppermute | solution.py:357
  46.7 2.3 %prep.5 = (bf16[1024,1024]{1,0:T(8,128)(2,1)S(1)}, f32[512,256]{1,0:T(8,128)S(1)}) custom-call(s32[129]{0:T(256)S(1)} %get-tuple-element.389.tab.refs_0_, s32[8]{0:T(128)S(1)} %copy-done.21, bf16[8,512,512]{2,1,0:T(8,128)(2,1)S(1)} %copy-done.1, bf16[512,512]{1,0:T(8,128)(2,1)S(1)} %factor_pack.1.own_ref.refs_0_, ...), custom_call_target="tpu_custom_call" | custom-call | flops 200000000 | bytes 6000000 | tf_op jit(solution)/shard_map/prep/pallas_call | solution.py:504
  49.0 3.6 %mask_below.3.a1 = bf16[1024,4096]{1,0:T(8,128)(2,1)S(1)} custom-call(s32[32,64]{1,0:T(8,128)S(1)} %copy-done.4, bf16[2048,4096]{1,0:T(8,128)(2,1)} %a_ref.3), custom_call_target="tpu_custom_call" | custom-call | flops 400000000 | bytes 12000000 | tf_op jit(solution)/shard_map/mask_below/pallas_call | solution.py:370
  52.6 1.2 %collective-permute-done.21.refs_4_ = bf16[256,256]{1,0:T(8,128)(2,1)S(1)} collective-permute-done((bf16[256,256]{1,0:T(8,128)(2,1)S(1)}, bf16[256,256]{1,0:T(8,128)(2,1)S(1)}, u32[]{:S(2)}, u32[]{:S(2)}) %collective-permute-start.21) | collective-permute-done | bytes 131104 | tf_op jit(solution)/shard_map/ppermute | solution.py:357
  54.3 1.6 %collective-permute-start.27 = (bf16[512,256]{1,0:T(8,128)(2,1)S(1)}, bf16[512,256]{1,0:T(8,128)(2,1)S(1)}, u32[]{:S(2)}, u32[]{:S(2)}) collective-permute-start(bf16[512,256]{1,0:T(8,128)(2,1)S(1)} %get-tuple-element.420), channel_id=1, source_target_pairs={{0,1},{1,0},{2,3},{3,2},{4,5},{5,4},{6,7},{7,6},{8,9},{9,8},{10,11... | collective-permute-start | bytes 786440 | tf_op jit(solution)/shard_map/ppermute | solution.py:360
  55.9 1.8 %pair_solve.5 = (bf16[1024,256]{1,0:T(8,128)(2,1)S(1)}, bf16[512,256]{1,0:T(8,128)(2,1)S(1)}, bf16[256,256]{1,0:T(8,128)(2,1)S(1)}) custom-call(s32[129]{0:T(256)S(1)} %get-tuple-element.389.tab.refs_0_, bf16[512,256]{1,0:T(8,128)(2,1)S(1)} %get-tuple-element.401.refs_1_, bf16[512,256]{1,0:T(8,128)(2,1)S(1)} %collective-permute-done.20.refs_2_, ...), custom_call_target="tpu_custom_call" | custom-call | flops 300000000 | bytes 9000000 | tf_op jit(solution)/shard_map/pair_solve/pallas_call | solution.py:547
  58.3 1.4 %collective-permute-start.26 = (bf16[256,256]{1,0:T(8,128)(2,1)S(1)}, bf16[256,256]{1,0:T(8,128)(2,1)S(1)}, u32[]{:S(2)}, u32[]{:S(2)}) collective-permute-start(bf16[256,256]{1,0:T(8,128)(2,1)S(1)} %get-tuple-element.418), channel_id=1, source_target_pairs={{0,24},{4,28},{8,16},{12,20},{16,8},{20,12},{24,0},{28,4},{1,25},{... | collective-permute-start | bytes 393224 | tf_op jit(solution)/shard_map/ppermute | solution.py:357
  59.7 2.4 %prep.6 = (bf16[1024,1024]{1,0:T(8,128)(2,1)S(1)}, f32[512,256]{1,0:T(8,128)S(1)}) custom-call(s32[129]{0:T(256)S(1)} %get-tuple-element.389.tab.refs_0_, s32[8]{0:T(128)S(1)} %copy-done.21, bf16[8,512,512]{2,1,0:T(8,128)(2,1)S(1)} %copy-done.1, bf16[512,512]{1,0:T(8,128)(2,1)S(1)} %factor_pack.1.own_ref.refs_0_, ...), custom_call_target="tpu_custom_call" | custom-call | flops 200000000 | bytes 6000000 | tf_op jit(solution)/shard_map/prep/pallas_call | solution.py:504
  62.1 2.9 %rows_below.2.sums = f32[2048,256]{1,0:T(8,128)S(1)} custom-call(s32[8]{0:T(128)S(1)} %copy-done.21, bf16[1024,4096]{1,0:T(8,128)(2,1)S(1)} %mask_below.2.a0, bf16[1024,4096]{1,0:T(8,128)(2,1)S(1)} %mask_below.3.a1, bf16[1024,256]{1,0:T(8,128)(2,1)S(1)} %get-tuple-element.408.refs_8_.x0_ref.x0, bf16[1024,256]{1,0:T(8,128)(2,1)S(1)} %get-tuple-element.416.x1_ref.refs_9_.x1), custom_call_target="tpu_custom_call" | custom-call | flops 300000000 | bytes 9000000 | tf_op jit(solution)/shard_map/rows_below/pallas_call | solution.py:520
  65.0 1.9 %collective-permute-done.26.refs_4_ = bf16[256,256]{1,0:T(8,128)(2,1)S(1)} collective-permute-done((bf16[256,256]{1,0:T(8,128)(2,1)S(1)}, bf16[256,256]{1,0:T(8,128)(2,1)S(1)}, u32[]{:S(2)}, u32[]{:S(2)}) %collective-permute-start.26) | collective-permute-done | bytes 131104 | tf_op jit(solution)/shard_map/ppermute | solution.py:357
  67.4 2.9 %collective-permute-start.32 = (bf16[512,256]{1,0:T(8,128)(2,1)S(1)}, bf16[512,256]{1,0:T(8,128)(2,1)S(1)}, u32[]{:S(2)}, u32[]{:S(2)}) collective-permute-start(bf16[512,256]{1,0:T(8,128)(2,1)S(1)} %get-tuple-element.432), channel_id=1, source_target_pairs={{0,3},{1,2},{2,1},{3,0},{4,7},{5,6},{6,5},{7,4},{8,11},{9,10},{10,... | collective-permute-start | bytes 786440 | tf_op jit(solution)/shard_map/ppermute | solution.py:360
  70.2 1.8 %pair_solve.6 = (bf16[1024,256]{1,0:T(8,128)(2,1)S(1)}, bf16[512,256]{1,0:T(8,128)(2,1)S(1)}, bf16[256,256]{1,0:T(8,128)(2,1)S(1)}) custom-call(s32[129]{0:T(256)S(1)} %get-tuple-element.389.tab.refs_0_, bf16[512,256]{1,0:T(8,128)(2,1)S(1)} %get-tuple-element.417.refs_1_, bf16[512,256]{1,0:T(8,128)(2,1)S(1)} %collective-permute-done.25.refs_2_, ...), custom_call_target="tpu_custom_call" | custom-call | flops 300000000 | bytes 9000000 | tf_op jit(solution)/shard_map/pair_solve/pallas_call | solution.py:547
  72.8 2.3 %collective-permute-start.31 = (bf16[256,256]{1,0:T(8,128)(2,1)S(1)}, bf16[256,256]{1,0:T(8,128)(2,1)S(1)}, u32[]{:S(2)}, u32[]{:S(2)}) collective-permute-start(bf16[256,256]{1,0:T(8,128)(2,1)S(1)} %get-tuple-element.430), channel_id=1, source_target_pairs={{0,24},{4,28},{8,16},{12,20},{16,8},{20,12},{24,0},{28,4},{1,25},{... | collective-permute-start | bytes 393224 | tf_op jit(solution)/shard_map/ppermute | solution.py:357
  75.1 1.7 %prep.7.refs_6_ = bf16[1024,1024]{1,0:T(8,128)(2,1)S(1)} custom-call(s32[129]{0:T(256)S(1)} %get-tuple-element.389.tab.refs_0_, s32[8]{0:T(128)S(1)} %copy-done.21, bf16[8,512,512]{2,1,0:T(8,128)(2,1)S(1)} %copy-done.1, bf16[512,512]{1,0:T(8,128)(2,1)S(1)} %factor_pack.1.own_ref.refs_0_, bf16[512,512]{1,0:T(8,128)(2,1)S(1)} %collective-permute-done.3.other_ref.refs_1_, ...), custom_call_target="tpu_custom_call" | custom-call | flops 200000000 | bytes 6000000 | tf_op jit(solution)/shard_map/prep/pallas_call | solution.py:504
  77.5 2.1 %rows_below.3.base = f32[2048,256]{1,0:T(8,128)S(1)} custom-call(s32[8]{0:T(128)S(1)} %copy-done.21, bf16[1024,4096]{1,0:T(8,128)(2,1)S(1)} %mask_below.2.a0, bf16[1024,4096]{1,0:T(8,128)(2,1)S(1)} %mask_below.3.a1, bf16[1024,256]{1,0:T(8,128)(2,1)S(1)} %get-tuple-element.428.x_ref.x2, ...), custom_call_target="tpu_custom_call", output_to_operand_aliasing={{}: (4, {})} | custom-call | flops 300000000 | bytes 9000000 | tf_op jit(solution)/shard_map/rows_below/pallas_call | solution.py:520
  79.6 2.6 %collective-permute-done.31.refs_4_ = bf16[256,256]{1,0:T(8,128)(2,1)S(1)} collective-permute-done((bf16[256,256]{1,0:T(8,128)(2,1)S(1)}, bf16[256,256]{1,0:T(8,128)(2,1)S(1)}, u32[]{:S(2)}, u32[]{:S(2)}) %collective-permute-start.31) | collective-permute-done | bytes 131104 | tf_op jit(solution)/shard_map/ppermute | solution.py:357
  82.7 1.2 %collective-permute-done.34.refs_5_ = bf16[256,256]{1,0:T(8,128)(2,1)S(1)} collective-permute-done((bf16[256,256]{1,0:T(8,128)(2,1)S(1)}, bf16[256,256]{1,0:T(8,128)(2,1)S(1)}, u32[]{:S(2)}, u32[]{:S(2)}) %collective-permute-start.34) | collective-permute-done | bytes 131104 | tf_op jit(solution)/shard_map/ppermute | solution.py:357
  85.1 3.0 %last_rows.1 = (bf16[4096,256]{1,0:T(8,128)(2,1)}, bf16[2048,256]{1,0:T(8,128)(2,1)}) custom-call(s32[8]{0:T(128)S(1)} %copy-done.21, bf16[1024,4096]{1,0:T(8,128)(2,1)S(1)} %mask_below.2.a0, bf16[1024,4096]{1,0:T(8,128)(2,1)S(1)} %mask_below.3.a1, bf16[1024,256]{1,0:T(8,128)(2,1)S(1)} %get-tuple-element.408.refs_8_.x0_ref.x0, ...), custom_call_target="tpu_custom_call" | custom-call | flops 300000000 | bytes 9000000 | tf_op jit(solution)/shard_map/last_rows/pallas_call | solution.py:561
  (72 shorter events, 16.8 us)
Async XLA Ops:
  3.1 2.1 %collective-permute-start.3 = (bf16[512,512]{1,0:T(8,128)(2,1)S(1)}, bf16[512,512]{1,0:T(8,128)(2,1)S(1)}, u32[]{:S(2)}, u32[]{:S(2)}) collective-permute-start(bf16[512,512]{1,0:T(8,128)(2,1)S(1)} %factor_pack.1.own_ref.refs_0_), channel_id=1, source_target_pairs={{0,4},{4,0},{8,12},{12,8},{16,20},{20,16},{24,28},{28,24},{1,5},{5... | collective-permute-start | bytes 1572872 | tf_op jit(solution)/shard_map/ppermute | solution.py:357
  5.3 13.5 %collective-permute-start.4 = (bf16[512,4096]{1,0:T(8,128)(2,1)S(1)}, bf16[512,4096]{1,0:T(8,128)(2,1)S(1)}, u32[]{:S(2)}, u32[]{:S(2)}) collective-permute-start(bf16[512,4096]{1,0:T(8,128)(2,1)S(1)} %copy-done), channel_id=1, source_target_pairs={{0,4},{4,0},{8,12},{12,8},{16,20},{20,16},{24,28},{28,24},{1,5},{5... | collective-permute-start | bytes 12582920 | tf_op jit(solution)/shard_map/ppermute | solution.py:357
  5.7 15.7 %collective-permute-start.14 = (bf16[1024,512]{1,0:T(8,128)(2,1)S(1)}, bf16[1024,512]{1,0:T(8,128)(2,1)S(1)}, u32[]{:S(2)}, u32[]{:S(2)}) collective-permute-start(bf16[1024,512]{1,0:T(8,128)(2,1)S(1)} %chip_pack.1), channel_id=1, source_target_pairs={{0,8},{4,20},{8,0},{12,28},{16,24},{20,4},{24,16},{28,12},{1,9},{5... | collective-permute-start | bytes 3145736 | tf_op jit(solution)/shard_map/ppermute | solution.py:363
  8.4 8.0 %collective-permute-start.5 = (bf16[128,256]{1,0:T(8,128)(2,1)S(1)}, bf16[128,256]{1,0:T(8,128)(2,1)S(1)}, u32[]{:S(2)}, u32[]{:S(2)}) collective-permute-start(bf16[128,256]{1,0:T(8,128)(2,1)S(1)} %get-tuple-element.377), channel_id=1, source_target_pairs={{0,1},{1,0},{2,3},{3,2},{4,5},{5,4},{6,7},{7,6},{8,9},{9,8},{10,11... | collective-permute-start | bytes 196616 | tf_op jit(solution)/shard_map/ppermute | solution.py:360
  10.0 7.5 %collective-permute-start.6 = (bf16[128,256]{1,0:T(8,128)(2,1)S(1)}, bf16[128,256]{1,0:T(8,128)(2,1)S(1)}, u32[]{:S(2)}, u32[]{:S(2)}) collective-permute-start(bf16[128,256]{1,0:T(8,128)(2,1)S(1)} %get-tuple-element.378), channel_id=1, source_target_pairs={{0,2},{1,3},{2,0},{3,1},{4,6},{5,7},{6,4},{7,5},{8,10},{9,11},{10,... | collective-permute-start | bytes 196616 | tf_op jit(solution)/shard_map/ppermute | solution.py:360
  12.6 6.2 %collective-permute-start.7 = (bf16[128,256]{1,0:T(8,128)(2,1)S(1)}, bf16[128,256]{1,0:T(8,128)(2,1)S(1)}, u32[]{:S(2)}, u32[]{:S(2)}) collective-permute-start(bf16[128,256]{1,0:T(8,128)(2,1)S(1)} %get-tuple-element.379), channel_id=1, source_target_pairs={{0,3},{1,2},{2,1},{3,0},{4,7},{5,6},{6,5},{7,4},{8,11},{9,10},{10,... | collective-permute-start | bytes 196616 | tf_op jit(solution)/shard_map/ppermute | solution.py:360
  18.8 1.3 %collective-permute-start.8 = (bf16[128,256]{1,0:T(8,128)(2,1)S(1)}, bf16[128,256]{1,0:T(8,128)(2,1)S(1)}, u32[]{:S(2)}, u32[]{:S(2)}) collective-permute-start(bf16[128,256]{1,0:T(8,128)(2,1)S(1)} %get-tuple-element.803.refs_0_), channel_id=1, source_target_pairs={{0,4},{4,0},{8,12},{12,8},{16,20},{20,16},{24,28},{28,24},{1,5},{5... | collective-permute-start | bytes 196616 | tf_op jit(solution)/shard_map/ppermute | solution.py:357
  18.8 1.4 %collective-permute-start.9 = (bf16[128,256]{1,0:T(8,128)(2,1)S(1)}, bf16[128,256]{1,0:T(8,128)(2,1)S(1)}, u32[]{:S(2)}, u32[]{:S(2)}) collective-permute-start(bf16[128,256]{1,0:T(8,128)(2,1)S(1)} %collective-permute-done.5.refs_1_), channel_id=1, source_target_pairs={{0,4},{4,0},{8,12},{12,8},{16,20},{20,16},{24,28},{28,24},{1,5},{5... | collective-permute-start | bytes 196616 | tf_op jit(solution)/shard_map/ppermute | solution.py:357
  19.3 1.3 %collective-permute-start.10 = (bf16[128,256]{1,0:T(8,128)(2,1)S(1)}, bf16[128,256]{1,0:T(8,128)(2,1)S(1)}, u32[]{:S(2)}, u32[]{:S(2)}) collective-permute-start(bf16[128,256]{1,0:T(8,128)(2,1)S(1)} %collective-permute-done.6.refs_2_), channel_id=1, source_target_pairs={{0,4},{4,0},{8,12},{12,8},{16,20},{20,16},{24,28},{28,24},{1,5},{5... | collective-permute-start | bytes 196616 | tf_op jit(solution)/shard_map/ppermute | solution.py:357
  19.3 1.4 %collective-permute-start.11 = (bf16[128,256]{1,0:T(8,128)(2,1)S(1)}, bf16[128,256]{1,0:T(8,128)(2,1)S(1)}, u32[]{:S(2)}, u32[]{:S(2)}) collective-permute-start(bf16[128,256]{1,0:T(8,128)(2,1)S(1)} %collective-permute-done.7.refs_3_), channel_id=1, source_target_pairs={{0,4},{4,0},{8,12},{12,8},{16,20},{20,16},{24,28},{28,24},{1,5},{5... | collective-permute-start | bytes 196616 | tf_op jit(solution)/shard_map/ppermute | solution.py:357
  21.4 13.9 %collective-permute-start.15 = (bf16[512,512]{1,0:T(8,128)(2,1)S(1)}, bf16[512,512]{1,0:T(8,128)(2,1)S(1)}, u32[]{:S(2)}, u32[]{:S(2)}) collective-permute-start(bf16[512,512]{1,0:T(8,128)(2,1)S(1)} %take_half.1), channel_id=1, source_target_pairs={{0,16},{4,12},{8,24},{12,4},{16,0},{20,28},{24,8},{28,20},{1,17},{... | collective-permute-start | bytes 1572872 | tf_op jit(solution)/shard_map/ppermute | solution.py:366
  23.2 11.7 %collective-permute-start.12 = (bf16[512,256]{1,0:T(8,128)(2,1)S(1)}, bf16[512,256]{1,0:T(8,128)(2,1)S(1)}, u32[]{:S(2)}, u32[]{:S(2)}) collective-permute-start(bf16[512,256]{1,0:T(8,128)(2,1)S(1)} %get-tuple-element.384.refs_1_), channel_id=1, source_target_pairs={{0,8},{4,20},{8,0},{12,28},{16,24},{20,4},{24,16},{28,12},{1,9},{5... | collective-permute-start | bytes 786440 | tf_op jit(solution)/shard_map/ppermute | solution.py:363
  24.7 10.2 %collective-permute-start.13 = (bf16[256,256]{1,0:T(8,128)(2,1)S(1)}, bf16[256,256]{1,0:T(8,128)(2,1)S(1)}, u32[]{:S(2)}, u32[]{:S(2)}) collective-permute-start(bf16[256,256]{1,0:T(8,128)(2,1)S(1)} %get-tuple-element.390), channel_id=1, source_target_pairs={{0,24},{4,28},{8,16},{12,20},{16,8},{20,12},{24,0},{28,4},{1,25},{... | collective-permute-start | bytes 393224 | tf_op jit(solution)/shard_map/ppermute | solution.py:357
  35.4 4.8 %collective-permute-start.18 = (bf16[1024,512]{1,0:T(8,128)(2,1)S(1)}, bf16[1024,512]{1,0:T(8,128)(2,1)S(1)}, u32[]{:S(2)}, u32[]{:S(2)}) collective-permute-start(bf16[1024,512]{1,0:T(8,128)(2,1)S(1)} %collective-permute-done.14.x_ref.refs_2_), channel_id=1, source_target_pairs={{0,4},{4,0},{8,12},{12,8},{16,20},{20,16},{24,28},{28,24},{1,5},{5... | collective-permute-start | bytes 3145736 | tf_op jit(solution)/shard_map/ppermute | solution.py:357
  36.4 3.7 %collective-permute-start.19 = (bf16[512,512]{1,0:T(8,128)(2,1)S(1)}, bf16[512,512]{1,0:T(8,128)(2,1)S(1)}, u32[]{:S(2)}, u32[]{:S(2)}) collective-permute-start(bf16[512,512]{1,0:T(8,128)(2,1)S(1)} %collective-permute-done.15.refs_4_), channel_id=1, source_target_pairs={{0,4},{4,0},{8,12},{12,8},{16,20},{20,16},{24,28},{28,24},{1,5},{5... | collective-permute-start | bytes 1572872 | tf_op jit(solution)/shard_map/ppermute | solution.py:357
  36.4 5.4 %collective-permute-start.16 = (bf16[512,256]{1,0:T(8,128)(2,1)S(1)}, bf16[512,256]{1,0:T(8,128)(2,1)S(1)}, u32[]{:S(2)}, u32[]{:S(2)}) collective-permute-start(bf16[512,256]{1,0:T(8,128)(2,1)S(1)} %collective-permute-done.12.refs_2_), channel_id=1, source_target_pairs={{0,4},{4,0},{8,12},{12,8},{16,20},{20,16},{24,28},{28,24},{1,5},{5... | collective-permute-start | bytes 786440 | tf_op jit(solution)/shard_map/ppermute | solution.py:357
  36.9 4.9 %collective-permute-start.17 = (bf16[256,256]{1,0:T(8,128)(2,1)S(1)}, bf16[256,256]{1,0:T(8,128)(2,1)S(1)}, u32[]{:S(2)}, u32[]{:S(2)}) collective-permute-start(bf16[256,256]{1,0:T(8,128)(2,1)S(1)} %collective-permute-done.13.refs_4_), channel_id=1, source_target_pairs={{0,4},{4,0},{8,12},{12,8},{16,20},{20,16},{24,28},{28,24},{1,5},{5... | collective-permute-start | bytes 393224 | tf_op jit(solution)/shard_map/ppermute | solution.py:357
  37.1 15.5 %collective-permute-start.22 = (bf16[512,256]{1,0:T(8,128)(2,1)S(1)}, bf16[512,256]{1,0:T(8,128)(2,1)S(1)}, u32[]{:S(2)}, u32[]{:S(2)}) collective-permute-start(bf16[512,256]{1,0:T(8,128)(2,1)S(1)} %get-tuple-element.405), channel_id=1, source_target_pairs={{0,2},{1,3},{2,0},{3,1},{4,6},{5,7},{6,4},{7,5},{8,10},{9,11},{10,... | collective-permute-start | bytes 786440 | tf_op jit(solution)/shard_map/ppermute | solution.py:360
  43.6 10.2 %collective-permute-start.20 = (bf16[512,256]{1,0:T(8,128)(2,1)S(1)}, bf16[512,256]{1,0:T(8,128)(2,1)S(1)}, u32[]{:S(2)}, u32[]{:S(2)}) collective-permute-start(bf16[512,256]{1,0:T(8,128)(2,1)S(1)} %get-tuple-element.401.refs_1_), channel_id=1, source_target_pairs={{0,8},{4,20},{8,0},{12,28},{16,24},{20,4},{24,16},{28,12},{1,9},{5... | collective-permute-start | bytes 786440 | tf_op jit(solution)/shard_map/ppermute | solution.py:363
  44.3 9.5 %collective-permute-start.21 = (bf16[256,256]{1,0:T(8,128)(2,1)S(1)}, bf16[256,256]{1,0:T(8,128)(2,1)S(1)}, u32[]{:S(2)}, u32[]{:S(2)}) collective-permute-start(bf16[256,256]{1,0:T(8,128)(2,1)S(1)} %get-tuple-element.402), channel_id=1, source_target_pairs={{0,24},{4,28},{8,16},{12,20},{16,8},{20,12},{24,0},{28,4},{1,25},{... | collective-permute-start | bytes 393224 | tf_op jit(solution)/shard_map/ppermute | solution.py:357
  53.8 2.1 %collective-permute-start.23 = (bf16[512,256]{1,0:T(8,128)(2,1)S(1)}, bf16[512,256]{1,0:T(8,128)(2,1)S(1)}, u32[]{:S(2)}, u32[]{:S(2)}) collective-permute-start(bf16[512,256]{1,0:T(8,128)(2,1)S(1)} %collective-permute-done.20.refs_2_), channel_id=1, source_target_pairs={{0,4},{4,0},{8,12},{12,8},{16,20},{20,16},{24,28},{28,24},{1,5},{5... | collective-permute-start | bytes 786440 | tf_op jit(solution)/shard_map/ppermute | solution.py:357
  53.8 2.1 %collective-permute-start.24 = (bf16[256,256]{1,0:T(8,128)(2,1)S(1)}, bf16[256,256]{1,0:T(8,128)(2,1)S(1)}, u32[]{:S(2)}, u32[]{:S(2)}) collective-permute-start(bf16[256,256]{1,0:T(8,128)(2,1)S(1)} %collective-permute-done.21.refs_4_), channel_id=1, source_target_pairs={{0,4},{4,0},{8,12},{12,8},{16,20},{20,16},{24,28},{28,24},{1,5},{5... | collective-permute-start | bytes 393224 | tf_op jit(solution)/shard_map/ppermute | solution.py:357
  54.3 10.7 %collective-permute-start.27 = (bf16[512,256]{1,0:T(8,128)(2,1)S(1)}, bf16[512,256]{1,0:T(8,128)(2,1)S(1)}, u32[]{:S(2)}, u32[]{:S(2)}) collective-permute-start(bf16[512,256]{1,0:T(8,128)(2,1)S(1)} %get-tuple-element.420), channel_id=1, source_target_pairs={{0,1},{1,0},{2,3},{3,2},{4,5},{5,4},{6,7},{7,6},{8,9},{9,8},{10,11... | collective-permute-start | bytes 786440 | tf_op jit(solution)/shard_map/ppermute | solution.py:360
  57.7 9.2 %collective-permute-start.25 = (bf16[512,256]{1,0:T(8,128)(2,1)S(1)}, bf16[512,256]{1,0:T(8,128)(2,1)S(1)}, u32[]{:S(2)}, u32[]{:S(2)}) collective-permute-start(bf16[512,256]{1,0:T(8,128)(2,1)S(1)} %get-tuple-element.417.refs_1_), channel_id=1, source_target_pairs={{0,8},{4,20},{8,0},{12,28},{16,24},{20,4},{24,16},{28,12},{1,9},{5... | collective-permute-start | bytes 786440 | tf_op jit(solution)/shard_map/ppermute | solution.py:363
  58.3 8.6 %collective-permute-start.26 = (bf16[256,256]{1,0:T(8,128)(2,1)S(1)}, bf16[256,256]{1,0:T(8,128)(2,1)S(1)}, u32[]{:S(2)}, u32[]{:S(2)}) collective-permute-start(bf16[256,256]{1,0:T(8,128)(2,1)S(1)} %get-tuple-element.418), channel_id=1, source_target_pairs={{0,24},{4,28},{8,16},{12,20},{16,8},{20,12},{24,0},{28,4},{1,25},{... | collective-permute-start | bytes 393224 | tf_op jit(solution)/shard_map/ppermute | solution.py:357
  66.9 3.4 %collective-permute-start.28 = (bf16[512,256]{1,0:T(8,128)(2,1)S(1)}, bf16[512,256]{1,0:T(8,128)(2,1)S(1)}, u32[]{:S(2)}, u32[]{:S(2)}) collective-permute-start(bf16[512,256]{1,0:T(8,128)(2,1)S(1)} %collective-permute-done.25.refs_2_), channel_id=1, source_target_pairs={{0,4},{4,0},{8,12},{12,8},{16,20},{20,16},{24,28},{28,24},{1,5},{5... | collective-permute-start | bytes 786440 | tf_op jit(solution)/shard_map/ppermute | solution.py:357
  66.9 3.4 %collective-permute-start.29 = (bf16[256,256]{1,0:T(8,128)(2,1)S(1)}, bf16[256,256]{1,0:T(8,128)(2,1)S(1)}, u32[]{:S(2)}, u32[]{:S(2)}) collective-permute-start(bf16[256,256]{1,0:T(8,128)(2,1)S(1)} %collective-permute-done.26.refs_4_), channel_id=1, source_target_pairs={{0,4},{4,0},{8,12},{12,8},{16,20},{20,16},{24,28},{28,24},{1,5},{5... | collective-permute-start | bytes 393224 | tf_op jit(solution)/shard_map/ppermute | solution.py:357
  67.4 10.1 %collective-permute-start.32 = (bf16[512,256]{1,0:T(8,128)(2,1)S(1)}, bf16[512,256]{1,0:T(8,128)(2,1)S(1)}, u32[]{:S(2)}, u32[]{:S(2)}) collective-permute-start(bf16[512,256]{1,0:T(8,128)(2,1)S(1)} %get-tuple-element.432), channel_id=1, source_target_pairs={{0,3},{1,2},{2,1},{3,0},{4,7},{5,6},{6,5},{7,4},{8,11},{9,10},{10,... | collective-permute-start | bytes 786440 | tf_op jit(solution)/shard_map/ppermute | solution.py:360
  72.1 10.2 %collective-permute-start.30 = (bf16[512,256]{1,0:T(8,128)(2,1)S(1)}, bf16[512,256]{1,0:T(8,128)(2,1)S(1)}, u32[]{:S(2)}, u32[]{:S(2)}) collective-permute-start(bf16[512,256]{1,0:T(8,128)(2,1)S(1)} %get-tuple-element.429.refs_1_), channel_id=1, source_target_pairs={{0,8},{4,20},{8,0},{12,28},{16,24},{20,4},{24,16},{28,12},{1,9},{5... | collective-permute-start | bytes 786440 | tf_op jit(solution)/shard_map/ppermute | solution.py:363
  72.8 9.4 %collective-permute-start.31 = (bf16[256,256]{1,0:T(8,128)(2,1)S(1)}, bf16[256,256]{1,0:T(8,128)(2,1)S(1)}, u32[]{:S(2)}, u32[]{:S(2)}) collective-permute-start(bf16[256,256]{1,0:T(8,128)(2,1)S(1)} %get-tuple-element.430), channel_id=1, source_target_pairs={{0,24},{4,28},{8,16},{12,20},{16,8},{20,12},{24,0},{28,4},{1,25},{... | collective-permute-start | bytes 393224 | tf_op jit(solution)/shard_map/ppermute | solution.py:357
  82.2 1.7 %collective-permute-start.33 = (bf16[512,256]{1,0:T(8,128)(2,1)S(1)}, bf16[512,256]{1,0:T(8,128)(2,1)S(1)}, u32[]{:S(2)}, u32[]{:S(2)}) collective-permute-start(bf16[512,256]{1,0:T(8,128)(2,1)S(1)} %collective-permute-done.30.refs_2_), channel_id=1, source_target_pairs={{0,4},{4,0},{8,12},{12,8},{16,20},{20,16},{24,28},{28,24},{1,5},{5... | collective-permute-start | bytes 786440 | tf_op jit(solution)/shard_map/ppermute | solution.py:357
  82.2 1.7 %collective-permute-start.34 = (bf16[256,256]{1,0:T(8,128)(2,1)S(1)}, bf16[256,256]{1,0:T(8,128)(2,1)S(1)}, u32[]{:S(2)}, u32[]{:S(2)}) collective-permute-start(bf16[256,256]{1,0:T(8,128)(2,1)S(1)} %collective-permute-done.31.refs_4_), channel_id=1, source_target_pairs={{0,4},{4,0},{8,12},{12,8},{16,20},{20,16},{24,28},{28,24},{1,5},{5... | collective-permute-start | bytes 393224 | tf_op jit(solution)/shard_map/ppermute | solution.py:357
  (8 other events, 68.2 us)
